TPU v7x, 32 devices: a whole 2x2x4 slice. The times are simulated.
32 devices in a mesh: ctx: 8 (over z, y), fsdp: 4 (over x, core).
Axes of the slice: x: 2, y: 2, z: 4, core: 2. Of those that a mesh axis runs over, the one named last changes fastest.
Arguments:
- query_rows: bfloat16 [8192, 4096], P('ctx', 'fsdp'), may hold values from -6 to 6
- key_rows: bfloat16 [8192, 4096], P('ctx', 'fsdp'), may hold values from -6 to 6
- value_rows: bfloat16 [8192, 4096], P('ctx', 'fsdp'), may hold values from -25 to 25
- norm_gain: bfloat16 [4096], P('fsdp'), may hold values from 0.099609375 to 1.8984375
- out_grad: bfloat16 [8192, 4096], P('ctx', 'fsdp'), may hold values from -6 to 6
Outputs:
- attended: bfloat16 [8192, 4096], P('ctx', 'fsdp')
- query_grad: bfloat16 [8192, 4096], P('ctx', 'fsdp')
- key_grad: bfloat16 [8192, 4096], P('ctx', 'fsdp')
- value_grad: bfloat16 [8192, 4096], P('ctx', 'fsdp')
All inputs are finite; a program needn't handle non-finite values.
Results may differ from a plain program's by a relative error of at most 0.0058.
Values sent between devices are 32-bit elements; how exact they have to be, the bound alone decides.
No kernel may reach another device: no remote copies, remote signals or barrier semaphores. Data moves between devices by JAX's collectives and lax.ppermute only.
A program may use at most 128 MiB of HBM per device.

v0:
```python
import jax
import jax.numpy as jnp
from jax import lax
from jax.sharding import PartitionSpec as P

HEADS = 32
HEAD_DIM = 128


def earlier_states(local):
    mine = lax.axis_index("ctx")
    piece = lax.all_gather(local[None], "ctx", axis=0, tiled=True)
    rows = jnp.arange(piece.shape[0], dtype=jnp.int32)
    keep = rows < mine
    return jnp.sum(jnp.where(keep[:, None, None, None], piece, 0.0), 0)


def later_states(local):
    mine = lax.axis_index("ctx")
    piece = lax.all_gather(local[None], "ctx", axis=0, tiled=True)
    rows = jnp.arange(piece.shape[0], dtype=jnp.int32)
    keep = rows > mine
    return jnp.sum(jnp.where(keep[:, None, None, None], piece, 0.0), 0)


def shards(query_rows, key_rows, value_rows, norm_gain, out_grad):
    tokens, width = query_rows.shape
    heads = width // HEAD_DIM
    full_width = HEADS * HEAD_DIM
    shape3 = (tokens, heads, HEAD_DIM)
    queries = query_rows.reshape(shape3)
    keys_here = key_rows.reshape(shape3)
    values_here = value_rows.reshape(shape3)
    causal = jnp.arange(tokens)[:, None] >= jnp.arange(tokens)[None, :]
    f32 = jnp.float32
    bf16 = jnp.bfloat16
    local_state = jnp.einsum("shd,she->hde", keys_here, values_here, preferred_element_type=f32)
    prefix = earlier_states(local_state).astype(bf16)
    scores = jnp.einsum("thd,shd->hts", queries, keys_here, preferred_element_type=f32)
    probs = jnp.where(causal[None], scores, 0.0).astype(bf16)
    mixed = jnp.einsum("hts,she->the", probs, values_here, preferred_element_type=f32)
    mixed = mixed + jnp.einsum("thd,hde->the", queries, prefix, preferred_element_type=f32)
    mixed = mixed.reshape(tokens, width)
    gain = norm_gain.astype(f32)
    weighted = out_grad.astype(f32) * gain
    squares_local = jnp.sum(mixed * mixed, 1)
    squares = lax.psum(squares_local, "fsdp")
    inverse = lax.rsqrt(squares / full_width + 1e-06)
    attended = (mixed * inverse[:, None] * gain).astype(bf16)
    cross = lax.psum(jnp.sum(weighted * mixed, 1), "fsdp")
    factor = inverse * inverse * cross / full_width
    mixed_grad = (inverse[:, None] * (weighted - mixed * factor[:, None])).astype(bf16)
    mixed_grad = mixed_grad.reshape(shape3)
    grad_state = jnp.einsum("thd,the->hde", queries, mixed_grad, preferred_element_type=f32)
    suffix = later_states(grad_state).astype(bf16)
    score_grad = jnp.einsum("the,she->hts", mixed_grad, values_here, preferred_element_type=f32)
    score_grad = jnp.where(causal[None], score_grad, 0.0).astype(bf16)
    dquery = jnp.einsum("hts,shd->thd", score_grad, keys_here, preferred_element_type=f32)
    dquery = dquery + jnp.einsum("the,hde->thd", mixed_grad, prefix, preferred_element_type=f32)
    dkey = jnp.einsum("hts,thd->shd", score_grad, queries, preferred_element_type=f32)
    dkey = dkey + jnp.einsum("she,hde->shd", values_here, suffix, preferred_element_type=f32)
    dvalue = jnp.einsum("hts,the->she", probs, mixed_grad, preferred_element_type=f32)
    dvalue = dvalue + jnp.einsum("shd,hde->she", keys_here, suffix, preferred_element_type=f32)
    flat = (tokens, width)
    return (
        attended,
        dquery.reshape(flat).astype(bf16),
        dkey.reshape(flat).astype(bf16),
        dvalue.reshape(flat).astype(bf16),
    )


def solution(mesh):
    in_specs = (P("ctx", "fsdp"), P("ctx", "fsdp"), P("ctx", "fsdp"), P("fsdp"), P("ctx", "fsdp"))
    out_specs = (P("ctx", "fsdp"), P("ctx", "fsdp"), P("ctx", "fsdp"), P("ctx", "fsdp"))
    return jax.shard_map(shards, mesh=mesh, in_specs=in_specs, out_specs=out_specs, check_vma=False)
```

profile of v0, /device:TPU:0, one launch (start us, length us, event | category | flops | bytes accessed | tf_op | source)
XLA Modules:
  0.0 236.4 jit_solution(18079762414164281397)
XLA Ops:
  7.2 0.0 copy-start
  7.2 0.0 all-gather.5.cloned.1.call-start
  7.2 3.7 %copy.65 = bf16[128,8,8,128]{3,2,1,0:T(8,128)(2,1)} copy(bf16[128,8,8,128]{3,1,2,0:T(8,128)(2,1)} %bitcast.110) | data formatting | bytes 4194304
  10.9 4.1 %copy.37 = bf16[1024,8,128]{0,2,1:T(8,128)(2,1)} copy(bf16[1024,8,128]{2,1,0:T(8,128)(2,1)} %bitcast.109) | data formatting | bytes 4194304 | tf_op jit(solution)/shard_map/reshape | solution.py:32
  15.0 0.0 copy-start.8
  15.0 3.8 %fusion.7 = f32[8,128,128]{2,1,0:T(8,128)} fusion(bf16[1024,8,128]{0,2,1:T(8,128)(2,1)} %copy.37, bf16[1024,1024]{1,0:T(8,128)(2,1)} %param.7), kind=kOutput, calls=%fused_computation.21 | convolution fusion | flops 268435456 | bytes 4718592 | tf_op jit(solution)/shard_map/shd,she->hde/dot_general | solution.py:37
  18.8 0.0 all-gather.5.cloned.1.call-update
  18.8 0.0 all-gather.7.cloned.1.call-start
  18.9 0.0 copy-done.8
  18.9 0.3 iota_compare_fusion
  19.2 0.0 copy-done
  19.2 0.0 copy-start.6
  19.2 10.1 %select_convert_fusion.1 = bf16[8,1024,1024]{2,1,0:T(8,128)(2,1)} fusion(pred[1024,1024]{1,0:T(8,128)(4,1)S(1)} %iota_compare_fusion, bf16[1024,1024]{1,0:T(8,128)(2,1)} %param.6, bf16[1024,1024]{1,0:T(8,128)(2,1)S(1)} %copy-done), kind=kOutput, calls=%fused_computation.1 | convolution fusion | flops 2164260864 | bytes 22020096 | tf_op jit(solution)/shard_map/thd,shd->hts/dot_general | solution.py:39
  29.4 0.0 copy-done.6
  29.4 11.4 %fusion.2 = f32[8,1024,128]{1,2,0:T(8,128)} fusion(bf16[8,1024,1024]{2,1,0:T(8,128)(2,1)} %select_convert_fusion.1, bf16[1024,1024]{1,0:T(8,128)(2,1)S(1)} %copy-done.6), kind=kOutput, calls=%fused_computation.16 | convolution fusion | flops 2147483648 | bytes 23068672 | tf_op jit(solution)/shard_map/hts,she->the/dot_general | solution.py:41
  40.8 53.7 %all-gather.5.cloned.1.call-done = f32[64,128,128]{2,1,0:T(8,128)} async-done(((f32[8,128,128]{2,1,0:T(8,128)}), f32[64,128,128]{2,1,0:T(8,128)}) %all-gather.5.cloned.1.call-update) | async-done | bytes 4194320 | tf_op jit(solution)/shard_map/all_gather | solution.py:12
  94.5 0.0 copy-start.5
  94.5 2.9 %select_reduce_fusion.1 = bf16[8,128,128]{2,1,0:T(8,128)(2,1)S(1)} fusion(f32[8,8,128,128]{3,2,1,0:T(8,128)} %bitcast.113, pred[8]{0:T(512)(128)(4,1)S(1)} %iota_compare_fusion.2), kind=kLoop, calls=%fused_computation.14 | loop fusion | flops 1966080 | bytes 4456456 | tf_op jit(solution)/shard_map/reduce_sum | solution.py:15
  97.3 0.6 copy-done.5
  97.9 2.9 %multiply_reduce_fusion.1 = (f32[1024]{0:T(1024)S(1)}, f32[1024,8,128]{0,2,1:T(8,128)}) fusion(bf16[8,128,128]{2,1,0:T(8,128)(2,1)S(1)} %select_reduce_fusion.1, f32[8,1024,128]{1,2,0:T(8,128)S(1)} %copy-done.5, bf16[1024,1024]{1,0:T(8,128)(2,1)S(1)} %copy-done), kind=kOutput, calls=%fused_computation.13 | convolution fusion | flops 271580160 | bytes 10752000 | tf_op jit(solution)/shard_map/thd,hde->the/dot_general | solution.py:42
  100.9 5.4 %copy.41 = f32[1024,1024]{1,0:T(8,128)} copy(f32[1024,1024]{0,1:T(8,128)} %bitcast.107) | data formatting | bytes 8388608 | tf_op jit(solution)/shard_map/reshape | solution.py:43
  106.2 3.5 %multiply_reduce_fusion = f32[1024]{0:T(1024)S(1)} fusion(f32[1024,1024]{1,0:T(8,128)} %copy.41, bf16[1024,1024]{1,0:T(8,128)(2,1)} %param.9, f32[1024]{0:T(1024)S(1)} %convert_element_type.47), kind=kLoop, calls=%fused_computation.10 | loop fusion | flops 4193280 | bytes 6299648 | tf_op jit(solution)/shard_map/reduce_sum | solution.py:50
  109.7 6.0 %all-reduce = (f32[1024]{0:T(1024)S(1)}, f32[1024]{0:T(1024)S(1)}) all-reduce(f32[1024]{0:T(1024)S(1)} %get-tuple-element.18, f32[1024]{0:T(1024)S(1)} %multiply_reduce_fusion), channel_id=1, replica_groups=mesh['ctx'=8,'fsdp'=4] {'fsdp'}, use_global_device_ids=true, to_apply=%region_2.3 | all-reduce | flops 2048 | bytes 16384 | tf_op jit(solution)/shard_map/psum | solution.py:47
  115.7 4.8 %multiply_convert_fusion = (bf16[1024,1024]{1,0:T(8,128)(2,1)}, bf16[1024,1024]{1,0:T(8,128)(2,1)}) fusion(f32[1024,1024]{1,0:T(8,128)} %copy.41, bf16[1024,1024]{1,0:T(8,128)(2,1)} %param.9, f32[1024]{0:T(1024)S(1)} %get-tuple-element.16, f32[1024]{0:T(1024)S(1)} %convert_element_type.47, f32[1024]{0:T(1024)S(1)} %get-tuple-element.17), kind=kLoop, calls=%fused_computation.9 | loop fusion | flops 9437184 | bytes 10498048 | tf_op jit(solution)/shard_map/convert_element_type | solution.py:52
  120.5 4.0 %copy.61 = bf16[1024,1024]{0,1:T(8,128)(2,1)} copy(bf16[1024,1024]{1,0:T(8,128)(2,1)} %get-tuple-element.14) | data formatting | bytes 4194304 | tf_op jit(solution)/shard_map/reshape | solution.py:53
  124.4 3.1 %fusion.26 = f32[8,128,128]{1,2,0:T(8,128)} fusion(bf16[1024,8,128]{0,2,1:T(8,128)(2,1)} %bitcast.103, bf16[1024,1024]{1,0:T(8,128)(2,1)S(1)} %copy-done), kind=kOutput, calls=%fused_computation.40 | convolution fusion | flops 268435456 | bytes 4718592 | tf_op jit(solution)/shard_map/thd,the->hde/dot_general | solution.py:54
  127.6 2.0 copy.51
  129.6 0.0 all-gather.7.cloned.1.call-update
  129.6 0.0 copy-start.3
  129.6 10.7 %select_convert_fusion = bf16[8,1024,1024]{2,1,0:T(8,128)(2,1)} fusion(pred[1024,1024]{1,0:T(8,128)(4,1)S(1)} %iota_compare_fusion, bf16[1024,8,128]{0,2,1:T(8,128)(2,1)} %bitcast.104, bf16[1024,1024]{1,0:T(8,128)(2,1)} %param.7), kind=kOutput, calls=%fused_computation | convolution fusion | flops 2164260864 | bytes 22020096 | tf_op jit(solution)/shard_map/the,she->hts/dot_general | solution.py:56
  140.4 0.0 copy-done.3
  140.4 0.0 copy-start.1
  140.4 9.4 %fusion.33 = f32[8,1024,128]{1,2,0:T(8,128)S(1)} fusion(bf16[8,1024,1024]{2,1,0:T(8,128)(2,1)} %select_convert_fusion, bf16[1024,8,128]{0,2,1:T(8,128)(2,1)S(1)} %copy-done.3), kind=kOutput, calls=%fused_computation.49 | convolution fusion | flops 2147483648 | bytes 23068672 | tf_op jit(solution)/shard_map/hts,shd->thd/dot_general | solution.py:58
  149.8 0.0 copy-done.1
  149.8 2.0 fusion.1
  151.8 3.9 %copy.56 = bf16[1024,1024]{1,0:T(8,128)(2,1)} copy(bf16[1024,1024]{0,1:T(8,128)(2,1)} %bitcast.111) | data formatting | bytes 4194304
  155.7 10.7 %fusion.34 = f32[8,128,1024]{2,1,0:T(8,128)} fusion(bf16[1024,8,128]{0,2,1:T(8,128)(2,1)} %bitcast.105, bf16[8,1024,1024]{2,1,0:T(8,128)(2,1)} %select_convert_fusion.1), kind=kOutput, calls=%fused_computation.50 | convolution fusion | flops 2147483648 | bytes 23068672 | tf_op jit(solution)/shard_map/hts,the->she/dot_general | solution.py:62
  166.5 35.0 %all-gather.7.cloned.1.call-done = f32[64,128,128]{2,1,0:T(8,128)} async-done(((f32[8,128,128]{2,1,0:T(8,128)}), f32[64,128,128]{2,1,0:T(8,128)}) %all-gather.7.cloned.1.call-update) | async-done | bytes 4194320 | tf_op jit(solution)/shard_map/all_gather | solution.py:20
  201.5 0.0 copy-start.7
  201.5 2.9 %select_reduce_fusion = bf16[8,128,128]{2,1,0:T(8,128)(2,1)S(1)} fusion(f32[8,8,128,128]{3,2,1,0:T(8,128)} %bitcast.114, pred[8]{0:T(512)(128)(4,1)S(1)} %iota_compare_fusion.1), kind=kLoop, calls=%fused_computation.8 | loop fusion | flops 1966080 | bytes 4456456 | tf_op jit(solution)/shard_map/reduce_sum | solution.py:23
  204.3 0.0 copy-done.7
  204.3 0.0 copy-start.2
  204.3 0.0 copy-start.4
  204.3 2.9 %fusion.4 = f32[8,128,1024]{2,1,0:T(8,128)} fusion(bf16[8,128,128]{2,1,0:T(8,128)(2,1)S(1)} %select_reduce_fusion, bf16[1024,1024]{1,0:T(8,128)(2,1)S(1)} %copy-done.7), kind=kOutput, calls=%fused_computation.18 | convolution fusion | flops 268435456 | bytes 6553600 | tf_op jit(solution)/shard_map/she,hde->shd/dot_general | solution.py:61
  207.2 0.5 copy-done.2
  207.7 1.0 copy-done.4
  208.7 2.1 add_convert_fusion
  210.8 3.9 %copy.58 = bf16[1024,1024]{1,0:T(8,128)(2,1)} copy(bf16[1024,1024]{0,1:T(8,128)(2,1)} %bitcast.112) | data formatting | bytes 4194304
  214.8 10.8 %fusion = bf16[1024,8,128]{0,2,1:T(8,128)(2,1)} fusion(f32[8,128,1024]{2,1,0:T(8,128)} %fusion.4, bf16[8,1024,1024]{2,1,0:T(8,128)(2,1)} %select_convert_fusion, bf16[1024,1024]{1,0:T(8,128)(2,1)S(1)} %copy-done), kind=kOutput, calls=%fused_computation.3 | convolution fusion | flops 2149580800 | bytes 25165824 | tf_op jit(solution)/shard_map/hts,thd->shd/dot_general | solution.py:60
  225.6 3.9 %copy.57 = bf16[1024,1024]{1,0:T(8,128)(2,1)} copy(bf16[1024,1024]{0,1:T(8,128)(2,1)} %bitcast.108) | data formatting | bytes 4194304
  (4 shorter events, 0.0 us)
Async XLA Ops:
  7.2 12.1 %copy-start = (bf16[1024,1024]{1,0:T(8,128)(2,1)S(1)}, bf16[1024,1024]{1,0:T(8,128)(2,1)}, u32[]{:S(2)}) copy-start(bf16[1024,1024]{1,0:T(8,128)(2,1)} %param.5) | copy-start | bytes 6291460
  7.2 87.3 %all-gather.5.cloned.1.call-start = ((), (), s32[]{:S(2)}) async-start(), calls=%async_computation | async-start | bytes 4718592 | tf_op jit(solution)/shard_map/all_gather | solution.py:12
  15.0 3.9 %copy-start.8 = (bf16[1024]{0:T(1024)(128)(2,1)S(1)}, bf16[1024]{0:T(1024)(128)(2,1)}, u32[]{:S(2)}) copy-start(bf16[1024]{0:T(1024)(128)(2,1)} %param.8) | copy-start | bytes 6148
  18.8 182.6 %all-gather.7.cloned.1.call-start = ((), (), s32[]{:S(2)}) async-start(), calls=%async_computation.1 | async-start | bytes 4718592 | tf_op jit(solution)/shard_map/all_gather | solution.py:20
  19.2 10.2 %copy-start.6 = (bf16[1024,1024]{1,0:T(8,128)(2,1)S(1)}, bf16[1024,1024]{1,0:T(8,128)(2,1)}, u32[]{:S(2)}) copy-start(bf16[1024,1024]{1,0:T(8,128)(2,1)} %param.7) | copy-start | bytes 6291460
  94.5 3.4 %copy-start.5 = (f32[8,1024,128]{1,2,0:T(8,128)S(1)}, f32[8,1024,128]{1,2,0:T(8,128)}, u32[]{:S(2)}) copy-start(f32[8,1024,128]{1,2,0:T(8,128)} %fusion.2) | copy-start | bytes 12582916
  129.6 10.7 %copy-start.3 = (bf16[1024,8,128]{0,2,1:T(8,128)(2,1)S(1)}, bf16[1024,8,128]{0,2,1:T(8,128)(2,1)}, u32[]{:S(2)}) copy-start(bf16[1024,8,128]{0,2,1:T(8,128)(2,1)} %copy.37) | copy-start | bytes 6291460
  140.4 9.4 %copy-start.1 = (bf16[1024,1024]{0,1:T(8,128)(2,1)S(1)}, bf16[1024,1024]{0,1:T(8,128)(2,1)}, u32[]{:S(2)}) copy-start(bf16[1024,1024]{0,1:T(8,128)(2,1)} %copy.61) | copy-start | bytes 6291460
  201.5 2.9 %copy-start.7 = (bf16[1024,1024]{1,0:T(8,128)(2,1)S(1)}, bf16[1024,1024]{1,0:T(8,128)(2,1)}, u32[]{:S(2)}) copy-start(bf16[1024,1024]{1,0:T(8,128)(2,1)} %param.7) | copy-start | bytes 6291460
  204.3 3.4 %copy-start.2 = (f32[8,128,1024]{2,1,0:T(8,128)S(1)}, f32[8,128,1024]{2,1,0:T(8,128)}, u32[]{:S(2)}) copy-start(f32[8,128,1024]{2,1,0:T(8,128)} %fusion.34) | copy-start | bytes 12582916
  204.3 4.4 %copy-start.4 = (bf16[1024,1024]{1,0:T(8,128)(2,1)S(1)}, bf16[1024,1024]{1,0:T(8,128)(2,1)}, u32[]{:S(2)}) copy-start(bf16[1024,1024]{1,0:T(8,128)(2,1)} %param.6) | copy-start | bytes 6291460
Sparse Core Ops, SparseCore 0:
  18.9 75.5 all-gather.4
  129.7 71.6 all-gather.6
where the time goes:
time: 237 us; the launch traced here: 236 us
  waiting for transfers between devices  88.7 us (37%)
  matrix products  80.1 us (34%)
  local copies, waits for them, and re-layouts  33.1 us (14%)
  other arithmetic  14.3 us (6%)
  between operations  14.2 us (6%)
  blocking collectives  5.95 us (3%)
    all_gather x1, waiting for transfers between devices, earlier_states(): piece = lax.all_gather(local[None], 'ctx', axis=0, tiled=True)  53.7 us
    all_gather x1, waiting for transfers between devices, later_states(): piece = lax.all_gather(local[None], 'ctx', axis=0, tiled=True)  35 us
    unnamed x22, local copies, waits for them, and re-layouts  17.6 us
    dot_general x1, matrix products, shards(): jnp.einsum('hts,she->the', probs, values_here, preferred_element_type=f32)  11.4 us
    dot_general x1, matrix products, shards(): jnp.einsum('hts,thd->shd', score_grad, queries, preferred_element_type=f32)  10.8 us
    dot_general x1, matrix products, shards(): jnp.einsum('hts,the->she', probs, mixed_grad, preferred_element_type=f32)  10.7 us
    dot_general x1, matrix products, shards(): jnp.einsum('the,she->hts', mixed_grad, values_here, preferred_element_typ...  10.7 us
    dot_general x1, matrix products, shards(): jnp.einsum('thd,shd->hts', queries, keys_here, preferred_element_type=f32)  10.1 us
  transfers between devices with their start and end apart: 2, of which 2 were waited for; matrix products, arithmetic and copies ran while one was open for 25% of the time, Pallas kernels for 0%

commit v1 on v0

v1 whole, which is shorter than its diff:
```python
import functools

import jax
import jax.numpy as jnp
from jax import lax
from jax.experimental import pallas as pl
from jax.experimental.pallas import tpu as pltpu
from jax.sharding import PartitionSpec as P

HEADS = 32
HEAD_DIM = 128
GROUP = 4
CHUNK = 256

F32 = jnp.float32
BF16 = jnp.bfloat16
D = HEAD_DIM


def nn(a, b):
    return lax.dot_general(a, b, (((1,), (0,)), ((), ())), preferred_element_type=F32)


def nt(a, b):
    return lax.dot_general(a, b, (((1,), (1,)), ((), ())), preferred_element_type=F32)


def tn(a, b):
    return lax.dot_general(a, b, (((0,), (0,)), ((), ())), preferred_element_type=F32)


def head_cols(quarter, j, per):
    return pl.ds(pl.multiple_of((quarter * per + j) * D, D), D)


def call(kernel, name, outs, args, flops, scratch=(), hbm_outs=0, vmem=8):
    def spec(x):
        if x.dtype == jnp.int32:
            return pl.BlockSpec(memory_space=pltpu.SMEM)
        return pl.BlockSpec(memory_space=pltpu.VMEM)

    size = sum(x.size * x.dtype.itemsize for x in args)
    return pl.pallas_call(
        kernel,
        name=name,
        out_shape=outs,
        in_specs=[spec(x) for x in args],
        out_specs=[pl.BlockSpec(memory_space=pltpu.VMEM) for _ in outs],
        scratch_shapes=list(scratch),
        cost_estimate=pl.CostEstimate(flops=flops, bytes_accessed=size, transcendentals=0),
        compiler_params=pltpu.CompilerParams(vmem_limit_bytes=vmem << 20),
    )(*args)


def state_kernel(slots, per, me_ref, a_ref, b_ref, *out_refs):
    me = me_ref[0]
    for s, out_ref in zip(slots, out_refs):
        for j in range(per):
            cols = head_cols(me ^ s, j, per)
            out_ref[pl.ds(j * D, D), :] = tn(a_ref[:, cols], b_ref[:, cols])


def intra_kernel(q_ref, k_ref, v_ref, mixed_ref, qt_ref):
    tokens, width = q_ref.shape
    row = lax.broadcasted_iota(jnp.int32, (CHUNK, CHUNK), 0)
    col = lax.broadcasted_iota(jnp.int32, (CHUNK, CHUNK), 1)
    causal = row >= col

    @pl.loop(0, width // D)
    def _(h):
        cols = pl.ds(pl.multiple_of(h * D, D), D)
        state = jnp.zeros((D, D), F32)
        for c in range(tokens // CHUNK):
            rows = pl.ds(c * CHUNK, CHUNK)
            q, k, v = q_ref[rows, cols], k_ref[rows, cols], v_ref[rows, cols]
            probs = jnp.where(causal, nt(q, k), 0.0).astype(BF16)
            out = nn(probs, v)
            if c > 0:
                out = out + nn(q, state.astype(BF16))
            mixed_ref[rows, cols] = out
            if (c + 1) * CHUNK < tokens:
                state = state + tn(k, v)
            qt_ref[cols, rows] = q.T


def mix_kernel(per, me_ref, q_ref, intra_ref, dy_ref, gain_ref, e0, e1, e2, e3, mixed_ref, red_ref, sq, cr):
    tokens = q_ref.shape[0]
    me = me_ref[0]
    first = True
    for s, e_ref in enumerate((e0, e1, e2, e3)):
        for j in range(per):
            cols = head_cols(me ^ s, j, per)
            prefix = e_ref[pl.ds(j * D, D), :].astype(BF16)
            gain = gain_ref[:, cols].astype(F32)
            for c in range(tokens // CHUNK):
                rows = pl.ds(c * CHUNK, CHUNK)
                mixed = intra_ref[rows, cols] + nn(q_ref[rows, cols], prefix)
                mixed_ref[rows, cols] = mixed
                weighted = dy_ref[rows, cols].astype(F32) * gain
                if first:
                    sq[rows, :] = mixed * mixed
                    cr[rows, :] = weighted * mixed
                else:
                    sq[rows, :] += mixed * mixed
                    cr[rows, :] += weighted * mixed
            first = False
    ones = jnp.ones((8, D), F32)
    dims = (((1,), (1,)), ((), ()))
    for i, acc in enumerate((sq, cr)):
        total = lax.dot_general(ones, acc[...], dims, precision=lax.Precision.HIGHEST, preferred_element_type=F32)
        red_ref[pl.ds(i, 1), :] = total[:1]


def row_scales(red_ref, full_width):
    inverse = lax.rsqrt(red_ref[0:1, :] / full_width + 1e-06)
    factor = inverse * inverse * red_ref[1:2, :] / full_width
    return inverse, factor


def spread(row):
    return jnp.broadcast_to(row, (D, row.shape[1])).T


def grad_kernel(slots, per, full_width, me_ref, qt_ref, mixed_ref, dy_ref, gain_ref, red_ref, mg_ref, *out_refs):
    tokens = mixed_ref.shape[0]
    me = me_ref[0]
    inverse, factor = row_scales(red_ref, full_width)
    inverse, factor = spread(inverse), spread(factor)
    for s, out_ref in zip(slots, out_refs):
        for j in range(per):
            cols = head_cols(me ^ s, j, per)
            gain = gain_ref[:, cols].astype(F32)
            state = jnp.zeros((D, D), F32)
            for c in range(tokens // CHUNK):
                rows = pl.ds(c * CHUNK, CHUNK)
                part = slice(c * CHUNK, (c + 1) * CHUNK)
                weighted = dy_ref[rows, cols].astype(F32) * gain
                mg = (inverse[part] * (weighted - mixed_ref[rows, cols] * factor[part])).astype(BF16)
                mg_ref[rows, cols] = mg
                state = state + nn(qt_ref[cols, rows], mg)
            out_ref[pl.ds(j * D, D), :] = state


def query_kernel(per, full_width, me_ref, k_ref, v_ref, mg_ref, mixed_ref, gain_ref, red_ref, e0, e1, e2, e3, att_ref, dq_ref):
    tokens, width = k_ref.shape
    me = me_ref[0]
    row = lax.broadcasted_iota(jnp.int32, (CHUNK, CHUNK), 0)
    col = lax.broadcasted_iota(jnp.int32, (CHUNK, CHUNK), 1)
    causal = row >= col
    inverse, _ = row_scales(red_ref, full_width)
    inverse = spread(inverse)
    for s, e_ref in enumerate((e0, e1, e2, e3)):
        for j in range(per):
            cols = head_cols(me ^ s, j, per)
            gain = gain_ref[:, cols].astype(F32)
            state = e_ref[pl.ds(j * D, D), :]
            for c in range(tokens // CHUNK):
                rows = pl.ds(c * CHUNK, CHUNK)
                part = slice(c * CHUNK, (c + 1) * CHUNK)
                k, v, mg = k_ref[rows, cols], v_ref[rows, cols], mg_ref[rows, cols]
                ds = jnp.where(causal, nt(mg, v), 0.0).astype(BF16)
                dq_ref[rows, cols] = (nn(ds, k) + nt(mg, state.astype(BF16))).astype(BF16)
                att_ref[rows, cols] = (mixed_ref[rows, cols] * inverse[part] * gain).astype(BF16)
                if (c + 1) * CHUNK < tokens:
                    state = state + tn(k, v)


def keyvalue_kernel(q_ref, k_ref, v_ref, qt_ref, mg_ref, dk_ref, dv_ref):
    tokens, width = q_ref.shape
    row = lax.broadcasted_iota(jnp.int32, (CHUNK, CHUNK), 0)
    col = lax.broadcasted_iota(jnp.int32, (CHUNK, CHUNK), 1)
    causal = row <= col

    @pl.loop(0, width // D)
    def _(h):
        cols = pl.ds(pl.multiple_of(h * D, D), D)
        state = jnp.zeros((D, D), F32)
        for c in reversed(range(tokens // CHUNK)):
            rows = pl.ds(c * CHUNK, CHUNK)
            q, k, v, mg = q_ref[rows, cols], k_ref[rows, cols], v_ref[rows, cols], mg_ref[rows, cols]
            probs = jnp.where(causal, nt(k, q), 0.0).astype(BF16)
            ds = jnp.where(causal, nt(v, mg), 0.0).astype(BF16)
            dk, dv = nn(ds, q), nn(probs, mg)
            if (c + 1) * CHUNK < tokens:
                later = state.astype(BF16)
                dk = dk + nt(v, later)
                dv = dv + nn(k, later)
            dk_ref[rows, cols] = dk
            dv_ref[rows, cols] = dv
            if c > 0:
                state = state + nn(qt_ref[cols, rows], mg)


def finish_kernel(per, me_ref, k_ref, v_ref, dki_ref, dvi_ref, e0, e1, e2, e3, dk_ref, dv_ref):
    tokens = k_ref.shape[0]
    me = me_ref[0]
    for s, e_ref in enumerate((e0, e1, e2, e3)):
        for j in range(per):
            cols = head_cols(me ^ s, j, per)
            suffix = e_ref[pl.ds(j * D, D), :].astype(BF16)
            for c in range(tokens // CHUNK):
                rows = pl.ds(c * CHUNK, CHUNK)
                dk_ref[rows, cols] = (dki_ref[rows, cols] + nt(v_ref[rows, cols], suffix)).astype(BF16)
                dv_ref[rows, cols] = (dvi_ref[rows, cols] + nn(k_ref[rows, cols], suffix)).astype(BF16)


def swap(x, n, mask):
    return lax.ppermute(x, "ctx", [(i, i ^ mask) for i in range(n)])


def scan_states(slots, me, n, ahead):
    low = me & (GROUP - 1)
    got = [slots[0]] + [swap(slots[s], n, s) for s in range(1, GROUP)]

    def before(a, b):
        return (a < b) if ahead else (a > b)

    total = (got[0] + got[1]) + (got[2] + got[3])
    carry = None
    step = GROUP
    while step < n:
        other = swap(total, n, step)
        kept = jnp.where(before(me ^ step, me), other, 0.0)
        carry = kept if carry is None else carry + kept
        step *= 2
        if step < n:
            total = total + other
    sums = []
    for s in range(GROUP):
        mine = low ^ s
        part = carry
        for t in range(GROUP):
            if t != s:
                term = jnp.where(before(low ^ t, mine), got[t], 0.0)
                part = term if part is None else part + term
        sums.append(part)
    return [sums[0]] + [swap(sums[s], n, s) for s in range(1, GROUP)]


def shards(n, q, k, v, norm_gain, dy):
    tokens, width = q.shape
    heads = width // D
    per = heads // GROUP
    full_width = HEADS * D
    me = lax.axis_index("ctx").astype(jnp.int32)
    low = (me & (GROUP - 1)).reshape(1)
    gain = norm_gain.reshape(1, width)
    state = jax.ShapeDtypeStruct((per * D, D), F32)
    wide = jax.ShapeDtypeStruct((tokens, width), F32)
    narrow = jax.ShapeDtypeStruct((tokens, width), BF16)
    unit = 2 * tokens * D * D

    def states(slots):
        kernel = functools.partial(state_kernel, slots, per)
        return call(kernel, "state", [state] * len(slots), [low, k, v], unit * per * len(slots))

    s1, s2, s3 = states((1, 2, 3))
    (s0,) = states((0,))
    intra, qt = call(intra_kernel, "intra", [wide, jax.ShapeDtypeStruct((width, tokens), BF16)], [q, k, v], 6 * unit * heads)
    pre = scan_states([s0, s1, s2, s3], me, n, True)

    acc = pltpu.VMEM((tokens, D), F32)
    mixed, red = call(
        functools.partial(mix_kernel, per), "mix", [wide, jax.ShapeDtypeStruct((2, tokens), F32)],
        [low, q, intra, dy, gain] + pre, unit * heads, scratch=(acc, acc))
    red = lax.psum(red, "fsdp")

    mg, g1, g2, g3, g0 = call(
        functools.partial(grad_kernel, (1, 2, 3, 0), per, full_width), "grad", [narrow] + [state] * 4,
        [low, qt, mixed, dy, gain, red], unit * heads)
    dki, dvi = call(keyvalue_kernel, "keyvalue", [wide, wide], [q, k, v, qt, mg], 11 * unit * heads)
    att, dq = call(
        functools.partial(query_kernel, per, full_width), "query", [narrow, narrow],
        [low, k, v, mg, mixed, gain, red] + pre, 6 * unit * heads)
    suf = scan_states([g0, g1, g2, g3], me, n, False)
    dk, dv = call(
        functools.partial(finish_kernel, per), "finish", [narrow, narrow],
        [low, k, v, dki, dvi] + suf, 2 * unit * heads)
    return att, dq, dk, dv


def solution(mesh):
    in_specs = (P("ctx", "fsdp"), P("ctx", "fsdp"), P("ctx", "fsdp"), P("fsdp"), P("ctx", "fsdp"))
    out_specs = (P("ctx", "fsdp"),) * 4
    body = functools.partial(shards, mesh.shape["ctx"])
    return jax.shard_map(body, mesh=mesh, in_specs=in_specs, out_specs=out_specs, check_vma=False)
```

time: 237 us -> 100 us (0.42)
  matrix products: 80.1 us -> 0 us
  waiting for transfers between devices: 88.7 us -> 16.7 us
  Pallas kernels: 0 us -> 34.6 us
  starting transfers between devices: 0.08 us -> 20 us
  other arithmetic: 14.3 us -> 0.3 us
  between operations: 14.2 us -> 0.81 us
  local copies, waits for them, and re-layouts: 33.1 us -> 21.4 us
    all_gather x2 -> x0, waiting for transfers between devices: 88.7 us -> none  [the longest x1 53.7 us: earlier_states(): piece = lax.all_gather(local[None], 'ctx', axis=0, tiled=True)]
    dot_general x12 -> x0, matrix products: 80.1 us -> none  [the longest x1 11.4 us: shards(): jnp.einsum('hts,she->the', probs, values_here, preferred_element_type=f32)]
    pallas_call x0 -> x8, Pallas kernels: none -> 34.6 us  [call(): pl.pallas_call(kernel, name=name, out_shape=outs, in_specs=[spec(x) for x...]
    ppermute x0 -> x14, starting transfers between devices: none -> 20 us  [swap(): return lax.ppermute(x, 'ctx', [(i, i ^ mask) for i in range(n)])]
    ppermute x0 -> x14, waiting for transfers between devices: none -> 16.7 us  [swap(): return lax.ppermute(x, 'ctx', [(i, i ^ mask) for i in range(n)])]
    reshape x3 -> x1, local copies, waits for them, and re-layouts: 13.4 us -> 0.01 us  [shards(): gain = norm_gain.reshape(1, width)]
    reduce_sum x3 -> x0, other arithmetic: 9.18 us -> none  [the longest x1 3.48 us: shards(): cross = lax.psum(jnp.sum(weighted * mixed, 1), 'fsdp')]
    convert_element_type x2 -> x0, other arithmetic: 4.77 us -> none  [the longest x1 4.77 us: shards(): (inverse[:, None] * (weighted - mixed * factor[:, None])).astype(bf16)]
  transfers between devices with their start and end apart: 2 -> 14, of which waited for: 2 -> 7; matrix products, arithmetic and copies ran while one was open for 25% -> 0% of each run, Pallas kernels for 0% -> 24%
where the time goes in v1:
time: 100 us; the launch traced here: 99.7 us
  Pallas kernels  34.6 us (35%)
  local copies, waits for them, and re-layouts  21.4 us (21%)
  starting transfers between devices  20 us (20%)
  waiting for transfers between devices  16.7 us (17%)
  blocking collectives  5.92 us (6%)
    pallas_call x8, Pallas kernels, call(): pl.pallas_call(kernel, name=name, out_shape=outs, in_specs=[spec(x) for x...  34.6 us
    unnamed x40, local copies, waits for them, and re-layouts  21.4 us
    ppermute x14, starting transfers between devices, swap(): return lax.ppermute(x, 'ctx', [(i, i ^ mask) for i in range(n)])  20 us
    ppermute x14, waiting for transfers between devices, swap(): return lax.ppermute(x, 'ctx', [(i, i ^ mask) for i in range(n)])  16.7 us
    psum x1, blocking collectives, shards(): red = lax.psum(red, 'fsdp')  5.92 us
  transfers between devices with their start and end apart: 14, of which 7 were waited for; matrix products, arithmetic and copies ran while one was open for 0% of the time, Pallas kernels for 24%

profile of v1, /device:TPU:0, one launch (start us, length us, event | category | flops | bytes accessed | tf_op | source)
XLA Modules:
  0.0 99.7 jit_solution(16689680375597508839)
XLA Ops:
  0.6 0.0 copy-start
  0.6 1.6 %copy-done = bf16[1024,1024]{1,0:T(8,128)(2,1)S(1)} copy-done((bf16[1024,1024]{1,0:T(8,128)(2,1)S(1)}, bf16[1024,1024]{1,0:T(8,128)(2,1)}, u32[]{:S(2)}) %copy-start) | copy-done | bytes 2097176
  2.2 1.6 %copy-done.2 = bf16[1024,1024]{1,0:T(8,128)(2,1)S(1)} copy-done((bf16[1024,1024]{1,0:T(8,128)(2,1)S(1)}, bf16[1024,1024]{1,0:T(8,128)(2,1)}, u32[]{:S(2)}) %copy-start.2) | copy-done | bytes 2097176
  3.8 1.0 state.3
  4.8 3.1 %collective-permute-start = (f32[256,128]{1,0:T(8,128)S(1)}, f32[256,128]{1,0:T(8,128)S(1)}, u32[]{:S(2)}, u32[]{:S(2)}) collective-permute-start(f32[256,128]{1,0:T(8,128)S(1)} %get-tuple-element.24), channel_id=1, source_target_pairs={{0,4},{4,0},{8,12},{12,8},{16,20},{20,16},{24,28},{28,24},{1,5},{5... | collective-permute-start | bytes 393224 | tf_op jit(solution)/shard_map/ppermute | solution.py:208
  7.9 1.6 %collective-permute-start.1 = (f32[256,128]{1,0:T(8,128)S(1)}, f32[256,128]{1,0:T(8,128)S(1)}, u32[]{:S(2)}, u32[]{:S(2)}) collective-permute-start(f32[256,128]{1,0:T(8,128)S(1)} %get-tuple-element.25), channel_id=1, source_target_pairs={{0,8},{4,12},{8,0},{12,4},{16,24},{20,28},{24,16},{28,20},{1,9},{5... | collective-permute-start | bytes 393224 | tf_op jit(solution)/shard_map/ppermute | solution.py:208
  9.4 0.0 collective-permute-start.2
  9.4 0.4 state.2
  9.9 1.5 %collective-permute-done = f32[256,128]{1,0:T(8,128)S(1)} collective-permute-done((f32[256,128]{1,0:T(8,128)S(1)}, f32[256,128]{1,0:T(8,128)S(1)}, u32[]{:S(2)}, u32[]{:S(2)}) %collective-permute-start) | collective-permute-done | bytes 131104 | tf_op jit(solution)/shard_map/ppermute | solution.py:208
  11.4 2.9 %collective-permute-done.1 = f32[256,128]{1,0:T(8,128)S(1)} collective-permute-done((f32[256,128]{1,0:T(8,128)S(1)}, f32[256,128]{1,0:T(8,128)S(1)}, u32[]{:S(2)}, u32[]{:S(2)}) %collective-permute-start.1) | collective-permute-done | bytes 131104 | tf_op jit(solution)/shard_map/ppermute | solution.py:208
  14.2 1.2 %collective-permute-done.2 = f32[256,128]{1,0:T(8,128)S(1)} collective-permute-done((f32[256,128]{1,0:T(8,128)S(1)}, f32[256,128]{1,0:T(8,128)S(1)}, u32[]{:S(2)}, u32[]{:S(2)}) %collective-permute-start.2) | collective-permute-done | bytes 131104 | tf_op jit(solution)/shard_map/ppermute | solution.py:208
  15.5 2.8 %collective-permute-start.3 = (f32[256,128]{1,0:T(8,128)S(1)}, f32[256,128]{1,0:T(8,128)S(1)}, u32[]{:S(2)}, u32[]{:S(2)}) collective-permute-start(f32[256,128]{1,0:T(8,128)S(1)} %add_add_fusion.1), channel_id=1, source_target_pairs={{0,16},{4,20},{8,24},{12,28},{16,0},{20,4},{24,8},{28,12},{1,17},{... | collective-permute-start | bytes 393224 | tf_op jit(solution)/shard_map/ppermute | solution.py:208
  18.3 0.0 copy-done.19
  18.3 5.4 %collective-permute-done.3 = f32[256,128]{1,0:T(8,128)S(1)} collective-permute-done((f32[256,128]{1,0:T(8,128)S(1)}, f32[256,128]{1,0:T(8,128)S(1)}, u32[]{:S(2)}, u32[]{:S(2)}) %collective-permute-start.3) | collective-permute-done | bytes 131104 | tf_op jit(solution)/shard_map/ppermute | solution.py:208
  23.7 0.1 select_add_fusion.4
  23.8 1.2 %collective-permute-start.6 = (f32[256,128]{1,0:T(8,128)S(1)}, f32[256,128]{1,0:T(8,128)S(1)}, u32[]{:S(2)}, u32[]{:S(2)}) collective-permute-start(f32[256,128]{1,0:T(8,128)S(1)} %get-tuple-element.44), channel_id=1, source_target_pairs={{0,12},{4,8},{8,4},{12,0},{16,28},{20,24},{24,20},{28,16},{1,13},{... | collective-permute-start | bytes 393224 | tf_op jit(solution)/shard_map/ppermute | solution.py:208
  25.0 1.3 %collective-permute-start.5 = (f32[256,128]{1,0:T(8,128)S(1)}, f32[256,128]{1,0:T(8,128)S(1)}, u32[]{:S(2)}, u32[]{:S(2)}) collective-permute-start(f32[256,128]{1,0:T(8,128)S(1)} %get-tuple-element.45), channel_id=1, source_target_pairs={{0,8},{4,12},{8,0},{12,4},{16,24},{20,28},{24,16},{28,20},{1,9},{5... | collective-permute-start | bytes 393224 | tf_op jit(solution)/shard_map/ppermute | solution.py:208
  26.3 1.0 %collective-permute-start.4 = (f32[256,128]{1,0:T(8,128)S(1)}, f32[256,128]{1,0:T(8,128)S(1)}, u32[]{:S(2)}, u32[]{:S(2)}) collective-permute-start(f32[256,128]{1,0:T(8,128)S(1)} %get-tuple-element.46), channel_id=1, source_target_pairs={{0,4},{4,0},{8,12},{12,8},{16,20},{20,16},{24,28},{28,24},{1,5},{5... | collective-permute-start | bytes 393224 | tf_op jit(solution)/shard_map/ppermute | solution.py:208
  27.4 0.0 copy-done.1
  27.4 1.6 %copy-done.3 = bf16[1024,1024]{1,0:T(8,128)(2,1)S(1)} copy-done((bf16[1024,1024]{1,0:T(8,128)(2,1)S(1)}, bf16[1024,1024]{1,0:T(8,128)(2,1)}, u32[]{:S(2)}) %copy-start.3) | copy-done | bytes 2097176
  29.0 1.6 %copy-done.11 = bf16[1024,1024]{1,0:T(8,128)(2,1)S(1)} copy-done((bf16[1024,1024]{1,0:T(8,128)(2,1)S(1)}, bf16[1024,1024]{1,0:T(8,128)(2,1)}, u32[]{:S(2)}) %copy-start.11) | copy-done | bytes 2097176
  30.6 6.3 %intra.1 = (f32[1024,1024]{1,0:T(8,128)S(1)}, bf16[1024,1024]{1,0:T(8,128)(2,1)S(1)}) custom-call(bf16[1024,1024]{1,0:T(8,128)(2,1)S(1)} %copy-done.11, bf16[1024,1024]{1,0:T(8,128)(2,1)S(1)} %copy-done.1, bf16[1024,1024]{1,0:T(8,128)(2,1)S(1)} %copy-done.3), custom_call_target="tpu_custom_call" | custom-call | flops 1610612736 | bytes 6291456 | tf_op jit(solution)/shard_map/intra/pallas_call | solution.py:43
  36.9 0.0 copy-start.13
  36.9 0.0 collective-permute-done.6.e3
  37.0 0.0 collective-permute-done.5.e2
  37.0 0.0 collective-permute-done.4.e1
  37.0 0.0 copy-done.9
  37.0 3.2 %mix.1 = (f32[1024,1024]{1,0:T(8,128)S(1)}, f32[2,1024]{1,0:T(2,128)S(1)}) custom-call(s32[1]{0:T(128)} %bitcast.me_ref, bf16[1024,1024]{1,0:T(8,128)(2,1)S(1)} %copy-done.11, f32[1024,1024]{1,0:T(8,128)S(1)} %get-tuple-element.23.intra_ref, bf16[1024,1024]{1,0:T(8,128)(2,1)S(1)} %copy-done.9, bf16[1,1024]{1,0:T(2,128)(2,1)S(1)} %reshape.15.gain_ref, ...), custom_call_target="tpu_custom_call" | custom-call | flops 268435456 | bytes 8914948 | tf_op jit(solution)/shard_map/mix/pallas_call | solution.py:43
  40.2 0.0 copy-done.13
  40.2 0.0 copy-start.6
  40.2 2.0 %copy-done.6 = f32[1024,1024]{1,0:T(8,128)} copy-done((f32[1024,1024]{1,0:T(8,128)}, f32[1024,1024]{1,0:T(8,128)S(1)}, u32[]{:S(2)}) %copy-start.6) | copy-done | bytes 4194328
  42.2 5.9 %psum.7.red_ref = f32[2,1024]{1,0:T(2,128)S(1)} all-reduce(f32[2,1024]{1,0:T(2,128)S(1)} %get-tuple-element.28), channel_id=1, replica_groups=mesh['ctx'=8,'fsdp'=4] {'fsdp'}, use_global_device_ids=true, to_apply=%region_0.1 | all-reduce | flops 2048 | bytes 16384 | tf_op jit(solution)/shard_map/psum | solution.py:266
  48.1 0.0 copy-start.7
  48.1 2.2 %copy-done.7 = f32[1024,1024]{1,0:T(8,128)S(1)} copy-done((f32[1024,1024]{1,0:T(8,128)S(1)}, f32[1024,1024]{1,0:T(8,128)}, u32[]{:S(2)}) %copy-start.7) | copy-done | bytes 4194328
  50.3 1.6 %copy-done.10 = bf16[1024,1024]{1,0:T(8,128)(2,1)S(1)} copy-done((bf16[1024,1024]{1,0:T(8,128)(2,1)S(1)}, bf16[1024,1024]{1,0:T(8,128)(2,1)}, u32[]{:S(2)}) %copy-start.10) | copy-done | bytes 2097176
  51.9 1.6 %copy-done.14 = bf16[1024,1024]{1,0:T(8,128)(2,1)S(1)} copy-done((bf16[1024,1024]{1,0:T(8,128)(2,1)S(1)}, bf16[1024,1024]{1,0:T(8,128)(2,1)}, u32[]{:S(2)}) %copy-start.14) | copy-done | bytes 2097176
  53.5 2.3 %grad.1 = (bf16[1024,1024]{1,0:T(8,128)(2,1)S(1)}, f32[256,128]{1,0:T(8,128)S(1)}, f32[256,128]{1,0:T(8,128)S(1)}, f32[256,128]{1,0:T(8,128)S(1)}, f32[256,128]{1,0:T(8,128)S(1)}) custom-call(s32[1]{0:T(128)} %bitcast.me_ref, bf16[1024,1024]{1,0:T(8,128)(2,1)S(1)} %copy-done.14, f32[1024,1024]{1,0:T(8,128)S(1)} %copy-done.7, ...), custom_call_target="tpu_custom_call" | custom-call | flops 268435456 | bytes 8398852 | tf_op jit(solution)/shard_map/grad/pallas_call | solution.py:43
  55.8 0.0 copy-start.16
  55.8 1.3 %copy-done.16 = bf16[1024,1024]{1,0:T(8,128)(2,1)} copy-done((bf16[1024,1024]{1,0:T(8,128)(2,1)}, bf16[1024,1024]{1,0:T(8,128)(2,1)S(1)}, u32[]{:S(2)}) %copy-start.16) | copy-done | bytes 2097176
  57.1 0.9 collective-permute-start.7
  58.1 0.7 collective-permute-start.8
  58.7 1.9 %collective-permute-start.9 = (f32[256,128]{1,0:T(8,128)S(1)}, f32[256,128]{1,0:T(8,128)S(1)}, u32[]{:S(2)}, u32[]{:S(2)}) collective-permute-start(f32[256,128]{1,0:T(8,128)S(1)} %get-tuple-element.37), channel_id=1, source_target_pairs={{0,12},{4,8},{8,4},{12,0},{16,28},{20,24},{24,20},{28,16},{1,13},{... | collective-permute-start | bytes 393224 | tf_op jit(solution)/shard_map/ppermute | solution.py:208
  60.6 2.0 %collective-permute-done.7 = f32[256,128]{1,0:T(8,128)S(1)} collective-permute-done((f32[256,128]{1,0:T(8,128)S(1)}, f32[256,128]{1,0:T(8,128)S(1)}, u32[]{:S(2)}, u32[]{:S(2)}) %collective-permute-start.7) | collective-permute-done | bytes 131104 | tf_op jit(solution)/shard_map/ppermute | solution.py:208
  62.6 1.8 %collective-permute-done.8 = f32[256,128]{1,0:T(8,128)S(1)} collective-permute-done((f32[256,128]{1,0:T(8,128)S(1)}, f32[256,128]{1,0:T(8,128)S(1)}, u32[]{:S(2)}, u32[]{:S(2)}) %collective-permute-start.8) | collective-permute-done | bytes 131104 | tf_op jit(solution)/shard_map/ppermute | solution.py:208
  64.4 1.9 %collective-permute-done.9 = f32[256,128]{1,0:T(8,128)S(1)} collective-permute-done((f32[256,128]{1,0:T(8,128)S(1)}, f32[256,128]{1,0:T(8,128)S(1)}, u32[]{:S(2)}, u32[]{:S(2)}) %collective-permute-start.9) | collective-permute-done | bytes 131104 | tf_op jit(solution)/shard_map/ppermute | solution.py:208
  66.4 1.9 %collective-permute-start.10 = (f32[256,128]{1,0:T(8,128)S(1)}, f32[256,128]{1,0:T(8,128)S(1)}, u32[]{:S(2)}, u32[]{:S(2)}) collective-permute-start(f32[256,128]{1,0:T(8,128)S(1)} %add_add_fusion), channel_id=1, source_target_pairs={{0,16},{4,20},{8,24},{12,28},{16,0},{20,4},{24,8},{28,12},{1,17},{... | collective-permute-start | bytes 393224 | tf_op jit(solution)/shard_map/ppermute | solution.py:208
  68.3 1.6 %copy-done.4 = bf16[1024,1024]{1,0:T(8,128)(2,1)S(1)} copy-done((bf16[1024,1024]{1,0:T(8,128)(2,1)S(1)}, bf16[1024,1024]{1,0:T(8,128)(2,1)}, u32[]{:S(2)}) %copy-start.4) | copy-done | bytes 2097176
  69.9 1.6 %copy-done.12 = bf16[1024,1024]{1,0:T(8,128)(2,1)S(1)} copy-done((bf16[1024,1024]{1,0:T(8,128)(2,1)S(1)}, bf16[1024,1024]{1,0:T(8,128)(2,1)}, u32[]{:S(2)}) %copy-start.12) | copy-done | bytes 2097176
  71.5 1.6 %copy-done.15 = bf16[1024,1024]{1,0:T(8,128)(2,1)S(1)} copy-done((bf16[1024,1024]{1,0:T(8,128)(2,1)S(1)}, bf16[1024,1024]{1,0:T(8,128)(2,1)}, u32[]{:S(2)}) %copy-start.15) | copy-done | bytes 2097176
  73.1 1.6 %copy-done.17 = bf16[1024,1024]{1,0:T(8,128)(2,1)S(1)} copy-done((bf16[1024,1024]{1,0:T(8,128)(2,1)S(1)}, bf16[1024,1024]{1,0:T(8,128)(2,1)}, u32[]{:S(2)}) %copy-start.17) | copy-done | bytes 2097176
  74.7 10.0 %keyvalue.1 = (f32[1024,1024]{1,0:T(8,128)S(1)}, f32[1024,1024]{1,0:T(8,128)S(1)}) custom-call(bf16[1024,1024]{1,0:T(8,128)(2,1)S(1)} %copy-done.12, bf16[1024,1024]{1,0:T(8,128)(2,1)S(1)} %copy-done.1, bf16[1024,1024]{1,0:T(8,128)(2,1)S(1)} %copy-done.4, bf16[1024,1024]{1,0:T(8,128)(2,1)S(1)} %copy-done.15, bf16[1024,1024]{1,0:T(8,128)(2,1)S(1)} %copy-done.17), custom_call_target="tpu_custom_call" | custom-call | flops 2952790016 | bytes 10485760 | tf_op jit(solution)/shard_map/keyvalue/pallas_call | solution.py:43
  84.7 0.0 collective-permute-done.10
  84.7 0.1 select_add_fusion
  84.8 2.7 %collective-permute-start.13 = (f32[256,128]{1,0:T(8,128)S(1)}, f32[256,128]{1,0:T(8,128)S(1)}, u32[]{:S(2)}, u32[]{:S(2)}) collective-permute-start(f32[256,128]{1,0:T(8,128)S(1)} %get-tuple-element.40), channel_id=1, source_target_pairs={{0,12},{4,8},{8,4},{12,0},{16,28},{20,24},{24,20},{28,16},{1,13},{... | collective-permute-start | bytes 393224 | tf_op jit(solution)/shard_map/ppermute | solution.py:208
  87.5 0.3 collective-permute-start.12
  87.8 0.6 collective-permute-start.11
  88.4 0.0 copy-done.5
  88.4 0.0 copy-done.8
  88.4 0.0 copy-done.18
  88.4 7.1 %query.1 = (bf16[1024,1024]{1,0:T(8,128)(2,1)}, bf16[1024,1024]{1,0:T(8,128)(2,1)}) custom-call(s32[1]{0:T(128)} %bitcast.me_ref, bf16[1024,1024]{1,0:T(8,128)(2,1)S(1)} %copy-done.1, bf16[1024,1024]{1,0:T(8,128)(2,1)S(1)} %copy-done.5, bf16[1024,1024]{1,0:T(8,128)(2,1)S(1)} %copy-done.18, f32[1024,1024]{1,0:T(8,128)S(1)} %copy-done.8, ...), custom_call_target="tpu_custom_call" | custom-call | flops 1610612736 | bytes 11020292 | tf_op jit(solution)/shard_map/query/pallas_call | solution.py:43
  95.5 0.0 collective-permute-done.13.e3
  95.5 0.0 collective-permute-done.12.e2
  95.5 0.0 collective-permute-done.11.e1
  95.5 4.2 %finish.1 = (bf16[1024,1024]{1,0:T(8,128)(2,1)}, bf16[1024,1024]{1,0:T(8,128)(2,1)}) custom-call(s32[1]{0:T(128)} %bitcast.me_ref, bf16[1024,1024]{1,0:T(8,128)(2,1)S(1)} %copy-done.1, bf16[1024,1024]{1,0:T(8,128)(2,1)S(1)} %copy-done.5, f32[1024,1024]{1,0:T(8,128)S(1)} %get-tuple-element.32.dki_ref, f32[1024,1024]{1,0:T(8,128)S(1)} %get-tuple-element.33.dvi_ref, ...), custom_call_target="tpu_custom_call" | custom-call | flops 536870912 | bytes 13107204 | tf_op jit(solution)/shard_map/finish/pallas_call | solution.py:43
  (18 shorter events, 0.1 us)
Async XLA Ops:
  0.6 1.6 %copy-start = (bf16[1024,1024]{1,0:T(8,128)(2,1)S(1)}, bf16[1024,1024]{1,0:T(8,128)(2,1)}, u32[]{:S(2)}) copy-start(bf16[1024,1024]{1,0:T(8,128)(2,1)} %k_ref.7) | copy-start | bytes 6291460
  2.2 1.6 %copy-start.2 = (bf16[1024,1024]{1,0:T(8,128)(2,1)S(1)}, bf16[1024,1024]{1,0:T(8,128)(2,1)}, u32[]{:S(2)}) copy-start(bf16[1024,1024]{1,0:T(8,128)(2,1)} %v_ref.7) | copy-start | bytes 6291460
  4.8 6.6 %collective-permute-start = (f32[256,128]{1,0:T(8,128)S(1)}, f32[256,128]{1,0:T(8,128)S(1)}, u32[]{:S(2)}, u32[]{:S(2)}) collective-permute-start(f32[256,128]{1,0:T(8,128)S(1)} %get-tuple-element.24), channel_id=1, source_target_pairs={{0,4},{4,0},{8,12},{12,8},{16,20},{20,16},{24,28},{28,24},{1,5},{5... | collective-permute-start | bytes 393224 | tf_op jit(solution)/shard_map/ppermute | solution.py:208
  7.9 6.4 %collective-permute-start.1 = (f32[256,128]{1,0:T(8,128)S(1)}, f32[256,128]{1,0:T(8,128)S(1)}, u32[]{:S(2)}, u32[]{:S(2)}) collective-permute-start(f32[256,128]{1,0:T(8,128)S(1)} %get-tuple-element.25), channel_id=1, source_target_pairs={{0,8},{4,12},{8,0},{12,4},{16,24},{20,28},{24,16},{28,20},{1,9},{5... | collective-permute-start | bytes 393224 | tf_op jit(solution)/shard_map/ppermute | solution.py:208
  9.4 8.8 %copy-start.19 = (bf16[1024]{0:T(1024)(128)(2,1)S(1)}, bf16[1024]{0:T(1024)(128)(2,1)}, u32[]{:S(2)}) copy-start(bf16[1024]{0:T(1024)(128)(2,1)} %param.8) | copy-start | bytes 6148
  9.4 18.0 %copy-start.1 = (bf16[1024,1024]{1,0:T(8,128)(2,1)S(1)}, bf16[1024,1024]{1,0:T(8,128)(2,1)}, u32[]{:S(2)}) copy-start(bf16[1024,1024]{1,0:T(8,128)(2,1)} %k_ref.7) | copy-start | bytes 6291460
  9.4 6.0 %collective-permute-start.2 = (f32[256,128]{1,0:T(8,128)S(1)}, f32[256,128]{1,0:T(8,128)S(1)}, u32[]{:S(2)}, u32[]{:S(2)}) collective-permute-start(f32[256,128]{1,0:T(8,128)S(1)} %get-tuple-element.26), channel_id=1, source_target_pairs={{0,12},{4,8},{8,4},{12,0},{16,28},{20,24},{24,20},{28,16},{1,13},{... | collective-permute-start | bytes 393224 | tf_op jit(solution)/shard_map/ppermute | solution.py:208
  15.5 8.3 %collective-permute-start.3 = (f32[256,128]{1,0:T(8,128)S(1)}, f32[256,128]{1,0:T(8,128)S(1)}, u32[]{:S(2)}, u32[]{:S(2)}) collective-permute-start(f32[256,128]{1,0:T(8,128)S(1)} %add_add_fusion.1), channel_id=1, source_target_pairs={{0,16},{4,20},{8,24},{12,28},{16,0},{20,4},{24,8},{28,12},{1,17},{... | collective-permute-start | bytes 393224 | tf_op jit(solution)/shard_map/ppermute | solution.py:208
  23.8 13.1 %collective-permute-start.6 = (f32[256,128]{1,0:T(8,128)S(1)}, f32[256,128]{1,0:T(8,128)S(1)}, u32[]{:S(2)}, u32[]{:S(2)}) collective-permute-start(f32[256,128]{1,0:T(8,128)S(1)} %get-tuple-element.44), channel_id=1, source_target_pairs={{0,12},{4,8},{8,4},{12,0},{16,28},{20,24},{24,20},{28,16},{1,13},{... | collective-permute-start | bytes 393224 | tf_op jit(solution)/shard_map/ppermute | solution.py:208
  25.0 12.0 %collective-permute-start.5 = (f32[256,128]{1,0:T(8,128)S(1)}, f32[256,128]{1,0:T(8,128)S(1)}, u32[]{:S(2)}, u32[]{:S(2)}) collective-permute-start(f32[256,128]{1,0:T(8,128)S(1)} %get-tuple-element.45), channel_id=1, source_target_pairs={{0,8},{4,12},{8,0},{12,4},{16,24},{20,28},{24,16},{28,20},{1,9},{5... | collective-permute-start | bytes 393224 | tf_op jit(solution)/shard_map/ppermute | solution.py:208
  26.3 10.6 %collective-permute-start.4 = (f32[256,128]{1,0:T(8,128)S(1)}, f32[256,128]{1,0:T(8,128)S(1)}, u32[]{:S(2)}, u32[]{:S(2)}) collective-permute-start(f32[256,128]{1,0:T(8,128)S(1)} %get-tuple-element.46), channel_id=1, source_target_pairs={{0,4},{4,0},{8,12},{12,8},{16,20},{20,16},{24,28},{28,24},{1,5},{5... | collective-permute-start | bytes 393224 | tf_op jit(solution)/shard_map/ppermute | solution.py:208
  27.4 1.6 %copy-start.3 = (bf16[1024,1024]{1,0:T(8,128)(2,1)S(1)}, bf16[1024,1024]{1,0:T(8,128)(2,1)}, u32[]{:S(2)}) copy-start(bf16[1024,1024]{1,0:T(8,128)(2,1)} %v_ref.7) | copy-start | bytes 6291460
  29.0 1.6 %copy-start.11 = (bf16[1024,1024]{1,0:T(8,128)(2,1)S(1)}, bf16[1024,1024]{1,0:T(8,128)(2,1)}, u32[]{:S(2)}) copy-start(bf16[1024,1024]{1,0:T(8,128)(2,1)} %q_ref.5) | copy-start | bytes 6291460
  30.6 6.4 %copy-start.9 = (bf16[1024,1024]{1,0:T(8,128)(2,1)S(1)}, bf16[1024,1024]{1,0:T(8,128)(2,1)}, u32[]{:S(2)}) copy-start(bf16[1024,1024]{1,0:T(8,128)(2,1)} %dy_ref.3) | copy-start | bytes 6291460
  36.9 3.3 %copy-start.13 = (bf16[1024,1024]{1,0:T(8,128)(2,1)}, bf16[1024,1024]{1,0:T(8,128)(2,1)S(1)}, u32[]{:S(2)}) copy-start(bf16[1024,1024]{1,0:T(8,128)(2,1)S(1)} %get-tuple-element.22.qt_ref) | copy-start | bytes 6291460
  40.2 2.0 %copy-start.6 = (f32[1024,1024]{1,0:T(8,128)}, f32[1024,1024]{1,0:T(8,128)S(1)}, u32[]{:S(2)}) copy-start(f32[1024,1024]{1,0:T(8,128)S(1)} %get-tuple-element.27.mixed_ref) | copy-start | bytes 12582916
  48.1 2.2 %copy-start.7 = (f32[1024,1024]{1,0:T(8,128)S(1)}, f32[1024,1024]{1,0:T(8,128)}, u32[]{:S(2)}) copy-start(f32[1024,1024]{1,0:T(8,128)} %copy-done.6) | copy-start | bytes 12582916
  50.3 1.6 %copy-start.10 = (bf16[1024,1024]{1,0:T(8,128)(2,1)S(1)}, bf16[1024,1024]{1,0:T(8,128)(2,1)}, u32[]{:S(2)}) copy-start(bf16[1024,1024]{1,0:T(8,128)(2,1)} %dy_ref.3) | copy-start | bytes 6291460
  51.9 1.6 %copy-start.14 = (bf16[1024,1024]{1,0:T(8,128)(2,1)S(1)}, bf16[1024,1024]{1,0:T(8,128)(2,1)}, u32[]{:S(2)}) copy-start(bf16[1024,1024]{1,0:T(8,128)(2,1)} %copy-done.13) | copy-start | bytes 6291460
  55.8 1.3 %copy-start.16 = (bf16[1024,1024]{1,0:T(8,128)(2,1)}, bf16[1024,1024]{1,0:T(8,128)(2,1)S(1)}, u32[]{:S(2)}) copy-start(bf16[1024,1024]{1,0:T(8,128)(2,1)S(1)} %get-tuple-element.29.mg_ref) | copy-start | bytes 6291460
  57.1 5.5 %collective-permute-start.7 = (f32[256,128]{1,0:T(8,128)S(1)}, f32[256,128]{1,0:T(8,128)S(1)}, u32[]{:S(2)}, u32[]{:S(2)}) collective-permute-start(f32[256,128]{1,0:T(8,128)S(1)} %get-tuple-element.35), channel_id=1, source_target_pairs={{0,4},{4,0},{8,12},{12,8},{16,20},{20,16},{24,28},{28,24},{1,5},{5... | collective-permute-start | bytes 393224 | tf_op jit(solution)/shard_map/ppermute | solution.py:208
  58.1 6.4 %collective-permute-start.8 = (f32[256,128]{1,0:T(8,128)S(1)}, f32[256,128]{1,0:T(8,128)S(1)}, u32[]{:S(2)}, u32[]{:S(2)}) collective-permute-start(f32[256,128]{1,0:T(8,128)S(1)} %get-tuple-element.36), channel_id=1, source_target_pairs={{0,8},{4,12},{8,0},{12,4},{16,24},{20,28},{24,16},{28,20},{1,9},{5... | collective-permute-start | bytes 393224 | tf_op jit(solution)/shard_map/ppermute | solution.py:208
  58.7 7.6 %collective-permute-start.9 = (f32[256,128]{1,0:T(8,128)S(1)}, f32[256,128]{1,0:T(8,128)S(1)}, u32[]{:S(2)}, u32[]{:S(2)}) collective-permute-start(f32[256,128]{1,0:T(8,128)S(1)} %get-tuple-element.37), channel_id=1, source_target_pairs={{0,12},{4,8},{8,4},{12,0},{16,28},{20,24},{24,20},{28,16},{1,13},{... | collective-permute-start | bytes 393224 | tf_op jit(solution)/shard_map/ppermute | solution.py:208
  66.4 18.3 %collective-permute-start.10 = (f32[256,128]{1,0:T(8,128)S(1)}, f32[256,128]{1,0:T(8,128)S(1)}, u32[]{:S(2)}, u32[]{:S(2)}) collective-permute-start(f32[256,128]{1,0:T(8,128)S(1)} %add_add_fusion), channel_id=1, source_target_pairs={{0,16},{4,20},{8,24},{12,28},{16,0},{20,4},{24,8},{28,12},{1,17},{... | collective-permute-start | bytes 393224 | tf_op jit(solution)/shard_map/ppermute | solution.py:208
  68.3 1.6 %copy-start.4 = (bf16[1024,1024]{1,0:T(8,128)(2,1)S(1)}, bf16[1024,1024]{1,0:T(8,128)(2,1)}, u32[]{:S(2)}) copy-start(bf16[1024,1024]{1,0:T(8,128)(2,1)} %v_ref.7) | copy-start | bytes 6291460
  69.9 1.6 %copy-start.12 = (bf16[1024,1024]{1,0:T(8,128)(2,1)S(1)}, bf16[1024,1024]{1,0:T(8,128)(2,1)}, u32[]{:S(2)}) copy-start(bf16[1024,1024]{1,0:T(8,128)(2,1)} %q_ref.5) | copy-start | bytes 6291460
  71.5 1.6 %copy-start.15 = (bf16[1024,1024]{1,0:T(8,128)(2,1)S(1)}, bf16[1024,1024]{1,0:T(8,128)(2,1)}, u32[]{:S(2)}) copy-start(bf16[1024,1024]{1,0:T(8,128)(2,1)} %copy-done.13) | copy-start | bytes 6291460
  73.1 1.6 %copy-start.17 = (bf16[1024,1024]{1,0:T(8,128)(2,1)S(1)}, bf16[1024,1024]{1,0:T(8,128)(2,1)}, u32[]{:S(2)}) copy-start(bf16[1024,1024]{1,0:T(8,128)(2,1)} %copy-done.16) | copy-start | bytes 6291460
  74.7 13.7 %copy-start.5 = (bf16[1024,1024]{1,0:T(8,128)(2,1)S(1)}, bf16[1024,1024]{1,0:T(8,128)(2,1)}, u32[]{:S(2)}) copy-start(bf16[1024,1024]{1,0:T(8,128)(2,1)} %v_ref.7) | copy-start | bytes 6291460
  74.7 13.7 %copy-start.8 = (f32[1024,1024]{1,0:T(8,128)S(1)}, f32[1024,1024]{1,0:T(8,128)}, u32[]{:S(2)}) copy-start(f32[1024,1024]{1,0:T(8,128)} %copy-done.6) | copy-start | bytes 12582916
  74.7 13.7 %copy-start.18 = (bf16[1024,1024]{1,0:T(8,128)(2,1)S(1)}, bf16[1024,1024]{1,0:T(8,128)(2,1)}, u32[]{:S(2)}) copy-start(bf16[1024,1024]{1,0:T(8,128)(2,1)} %copy-done.16) | copy-start | bytes 6291460
  84.8 10.6 %collective-permute-start.13 = (f32[256,128]{1,0:T(8,128)S(1)}, f32[256,128]{1,0:T(8,128)S(1)}, u32[]{:S(2)}, u32[]{:S(2)}) collective-permute-start(f32[256,128]{1,0:T(8,128)S(1)} %get-tuple-element.40), channel_id=1, source_target_pairs={{0,12},{4,8},{8,4},{12,0},{16,28},{20,24},{24,20},{28,16},{1,13},{... | collective-permute-start | bytes 393224 | tf_op jit(solution)/shard_map/ppermute | solution.py:208
  87.5 8.0 %collective-permute-start.12 = (f32[256,128]{1,0:T(8,128)S(1)}, f32[256,128]{1,0:T(8,128)S(1)}, u32[]{:S(2)}, u32[]{:S(2)}) collective-permute-start(f32[256,128]{1,0:T(8,128)S(1)} %get-tuple-element.41), channel_id=1, source_target_pairs={{0,8},{4,12},{8,0},{12,4},{16,24},{20,28},{24,16},{28,20},{1,9},{5... | collective-permute-start | bytes 393224 | tf_op jit(solution)/shard_map/ppermute | solution.py:208
  87.8 7.7 %collective-permute-start.11 = (f32[256,128]{1,0:T(8,128)S(1)}, f32[256,128]{1,0:T(8,128)S(1)}, u32[]{:S(2)}, u32[]{:S(2)}) collective-permute-start(f32[256,128]{1,0:T(8,128)S(1)} %get-tuple-element.42), channel_id=1, source_target_pairs={{0,4},{4,0},{8,12},{12,8},{16,20},{20,16},{24,28},{28,24},{1,5},{5... | collective-permute-start | bytes 393224 | tf_op jit(solution)/shard_map/ppermute | solution.py:208

commit v2 on v0

v2 whole, which is shorter than its diff:
```python
import functools

import jax
import jax.numpy as jnp
from jax import lax
from jax.experimental import pallas as pl
from jax.experimental.pallas import tpu as pltpu
from jax.sharding import PartitionSpec as P


HEADS = 32
HEAD_DIM = 128
GROUP = 4
CHUNK = 256
ROWS = 128

F32 = jnp.float32
BF16 = jnp.bfloat16
D = HEAD_DIM


def nn(a, b):
    return lax.dot_general(a, b, (((1,), (0,)), ((), ())), preferred_element_type=F32)


def nt(a, b):
    return lax.dot_general(a, b, (((1,), (1,)), ((), ())), preferred_element_type=F32)


def tn(a, b):
    return lax.dot_general(a, b, (((0,), (0,)), ((), ())), preferred_element_type=F32)


def slot_cols(me, s, wide):
    return pl.ds(pl.multiple_of((me ^ s) * wide, D), wide)


def head_cols(me, s, j, wide):
    return pl.ds(pl.multiple_of((me ^ s) * wide + j * D, D), D)


def diagonal(blocks):
    if len(blocks) == 1:
        return blocks[0]
    zero = jnp.zeros_like(blocks[0])
    lines = [jnp.concatenate([b if i == j else zero for j in range(len(blocks))], 1) for i, b in enumerate(blocks)]
    return jnp.concatenate(lines, 0)


def heads_of(ref, per):
    return [ref[pl.ds(j * D, D), :] for j in range(per)]


VMEM, HBM, SMEM = pltpu.VMEM, pltpu.HBM, pltpu.SMEM


def call(kernel, outs, args, flops, out_spaces=None, in_spaces=None, scratch=(), vmem=4):
    in_spaces = in_spaces or [SMEM if x.dtype == jnp.int32 else VMEM for x in args]
    out_spaces = out_spaces or [VMEM for _ in outs]
    size = sum(x.size * x.dtype.itemsize for x in args)
    return pl.pallas_call(
        kernel,
        out_shape=outs,
        in_specs=[pl.BlockSpec(memory_space=s) for s in in_spaces],
        out_specs=[pl.BlockSpec(memory_space=s) for s in out_spaces],
        scratch_shapes=list(scratch),
        cost_estimate=pl.CostEstimate(flops=flops, bytes_accessed=size, transcendentals=0),
        compiler_params=pltpu.CompilerParams(vmem_limit_bytes=vmem << 20),
    )(*args)


def state_kernel(per, me_ref, k_hbm, v_hbm, k_ref, v_ref, s1, s2, s3, sems):
    me = me_ref[0] & (GROUP - 1)
    copies = []
    for i, s in enumerate((1, 2, 3, 0)):
        cols = slot_cols(me, s, per * D)
        pair = [
            pltpu.make_async_copy(src.at[:, cols], dst.at[:, cols], sems.at[2 * i + n])
            for n, (src, dst) in enumerate(((k_hbm, k_ref), (v_hbm, v_ref)))
        ]
        for copy in pair:
            copy.start()
        copies.append(pair)
    for pair, s, out_ref in zip(copies, (1, 2, 3), (s1, s2, s3)):
        for copy in pair:
            copy.wait()
        for j in range(per):
            cols = head_cols(me, s, j, per * D)
            out_ref[pl.ds(j * D, D), :] = tn(k_ref[:, cols], v_ref[:, cols])
    for copy in copies[3]:
        copy.wait()


def own_kernel(per, me_ref, k_ref, v_ref, q_hbm, dy_hbm, s0, q_ref, dy_ref, sems):
    me = me_ref[0] & (GROUP - 1)
    copies = [
        pltpu.make_async_copy(q_hbm, q_ref, sems.at[0]),
        pltpu.make_async_copy(dy_hbm, dy_ref, sems.at[1]),
    ]
    for copy in copies:
        copy.start()
    for j in range(per):
        cols = head_cols(me, 0, j, per * D)
        s0[pl.ds(j * D, D), :] = tn(k_ref[:, cols], v_ref[:, cols])
    for copy in copies:
        copy.wait()


def lower_mask(transposed):
    row = lax.broadcasted_iota(jnp.int32, (CHUNK, CHUNK), 0)
    col = lax.broadcasted_iota(jnp.int32, (CHUNK, CHUNK), 1)
    return (row <= col) if transposed else (row >= col)


def intra_kernel(slots, per, me_ref, q_ref, k_ref, v_ref, mixed_ref, qt_ref, pt_ref, st_ref):
    tokens = q_ref.shape[0]
    me = me_ref[0] & (GROUP - 1)
    causal, upper = lower_mask(False), lower_mask(True)
    for i, s in enumerate(slots):
        for j in range(per):
            cols = head_cols(me, s, j, per * D)
            own = pl.ds((i * per + j) * D, D)
            state = jnp.zeros((D, D), F32)
            for c in range(tokens // CHUNK):
                rows = pl.ds(c * CHUNK, CHUNK)
                q, k, v = q_ref[rows, cols], k_ref[rows, cols], v_ref[rows, cols]
                probs = jnp.where(causal, nt(q, k), 0.0).astype(BF16)
                out = nn(probs, v)
                if c > 0:
                    out = out + nn(q, state.astype(BF16))
                mixed_ref[rows, own] = out
                pt_ref[i * per + j, rows, :] = jnp.where(upper, nt(k, q), 0.0).astype(BF16)
                qt_ref[own, rows] = q.T
                st_ref[i * per + j, pl.ds(c * D, D), :] = state
                if (c + 1) * CHUNK < tokens:
                    state = state + tn(k, v)


def mix_kernel(per, halves, me_ref, q_ref, dy_ref, gain_ref, e0, e1, e2, e3, in0, in1, mixed_ref, red_ref, sq, cr):
    tokens = q_ref.shape[0]
    me = me_ref[0] & (GROUP - 1)
    wide = per * D
    for s, e_ref in enumerate((e0, e1, e2, e3)):
        cols = slot_cols(me, s, wide)
        intra_ref = (in0, in1)[s // halves]
        own = pl.ds((s % halves) * wide, wide)
        prefix = diagonal([e.astype(BF16) for e in heads_of(e_ref, per)])
        gain = gain_ref[:, cols].astype(F32)
        for c in range(tokens // ROWS):
            rows = pl.ds(c * ROWS, ROWS)
            mixed = intra_ref[rows, own] + nn(q_ref[rows, cols], prefix)
            mixed_ref[rows, cols] = mixed
            weighted = dy_ref[rows, cols].astype(F32) * gain * mixed
            square = mixed * mixed
            square = sum(square[:, j * D:(j + 1) * D] for j in range(per))
            weighted = sum(weighted[:, j * D:(j + 1) * D] for j in range(per))
            if s == 0:
                sq[rows, :] = square
                cr[rows, :] = weighted
            else:
                sq[rows, :] += square
                cr[rows, :] += weighted
    ones = jnp.ones((8, D), F32)
    dims = (((1,), (1,)), ((), ()))
    for i, acc in enumerate((sq, cr)):
        total = lax.dot_general(ones, acc[...], dims, precision=lax.Precision.HIGHEST, preferred_element_type=F32)
        red_ref[pl.ds(i, 1), :] = total[:1]


def row_scales(red_ref, full_width):
    inverse = lax.rsqrt(red_ref[0:1, :] / full_width + 1e-06)
    factor = inverse * inverse * red_ref[1:2, :] / full_width
    return inverse, factor


def spread(row, c):
    return jnp.broadcast_to(row[:, c * ROWS:(c + 1) * ROWS], (D, ROWS)).T


def grad_kernel(per, halves, full_width, me_ref, qt0, qt1, mixed_ref, dy_ref, gain_ref, red_ref, mg_ref, g0, g1, g2, g3):
    tokens, width = mixed_ref.shape
    me = me_ref[0] & (GROUP - 1)
    inverse, factor = row_scales(red_ref, full_width)
    for c in range(tokens // ROWS):
        rows = pl.ds(c * ROWS, ROWS)
        inv, fac = spread(inverse, c), spread(factor, c)
        for h in range(width // D):
            cols = pl.ds(h * D, D)
            weighted = dy_ref[rows, cols].astype(F32) * gain_ref[:, cols].astype(F32)
            mg_ref[rows, cols] = (inv * (weighted - mixed_ref[rows, cols] * fac)).astype(BF16)
    for s in (1, 2, 3, 0):
        out_ref = (g0, g1, g2, g3)[s]
        for j in range(per):
            own = pl.ds(((s % halves) * per + j) * D, D)
            cols = head_cols(me, s, j, per * D)
            out_ref[pl.ds(j * D, D), :] = nn((qt0, qt1)[s // halves][own, :], mg_ref[:, cols])


def query_kernel(per, halves, full_width, me_ref, k_ref, v_ref, mg_ref, mixed_ref, gain_ref, red_ref, e0, e1, e2, e3, st0, st1, att_hbm, dq_hbm, att, dq, sems):
    tokens, width = k_ref.shape
    me = me_ref[0] & (GROUP - 1)
    wide = per * D
    causal = lower_mask(False)
    inverse, _ = row_scales(red_ref, full_width)
    for c in range(tokens // ROWS):
        rows = pl.ds(c * ROWS, ROWS)
        inv = spread(inverse, c)
        for h in range(width // D):
            cols = pl.ds(h * D, D)
            att[rows, cols] = (mixed_ref[rows, cols] * inv * gain_ref[:, cols].astype(F32)).astype(BF16)
    copies = [pltpu.make_async_copy(att, att_hbm, sems.at[GROUP])]
    copies[0].start()
    for s, e_ref in enumerate((e0, e1, e2, e3)):
        cols = slot_cols(me, s, wide)
        st_ref = (st0, st1)[s // halves]
        prefix = heads_of(e_ref, per)
        for c in range(tokens // CHUNK):
            rows = pl.ds(c * CHUNK, CHUNK)
            states = [prefix[j] + st_ref[(s % halves) * per + j, pl.ds(c * D, D), :] if c else prefix[j] for j in range(per)]
            far = nt(mg_ref[rows, cols], diagonal([x.astype(BF16) for x in states]))
            for j in range(per):
                one = head_cols(me, s, j, wide)
                ds = jnp.where(causal, nt(mg_ref[rows, one], v_ref[rows, one]), 0.0).astype(BF16)
                dq[rows, one] = (nn(ds, k_ref[rows, one]) + far[:, j * D:(j + 1) * D]).astype(BF16)
        copies.append(pltpu.make_async_copy(dq.at[:, cols], dq_hbm.at[:, cols], sems.at[s]))
        copies[-1].start()
    for copy in copies:
        copy.wait()


def keyvalue_kernel(slots, per, me_ref, q_ref, k_ref, v_ref, mg_ref, qt_ref, pt_ref, dk_ref, dv_ref):
    tokens = q_ref.shape[0]
    me = me_ref[0] & (GROUP - 1)
    wide = per * D
    upper = lower_mask(True)
    for i, s in enumerate(slots):
        pair = slot_cols(me, s, wide)
        states = [jnp.zeros((D, D), F32) for _ in range(per)]
        for c in reversed(range(tokens // CHUNK)):
            rows = pl.ds(c * CHUNK, CHUNK)
            last = (c + 1) * CHUNK == tokens
            if not last:
                later = diagonal([x.astype(BF16) for x in states])
                far_k = nt(v_ref[rows, pair], later)
                far_v = nn(k_ref[rows, pair], later)
            for j in range(per):
                own = pl.ds((i * per + j) * D, D)
                cols = head_cols(me, s, j, wide)
                mg = mg_ref[rows, cols]
                ds = jnp.where(upper, nt(v_ref[rows, cols], mg), 0.0).astype(BF16)
                dk = nn(ds, q_ref[rows, cols])
                dv = nn(pt_ref[i * per + j, rows, :], mg)
                if not last:
                    dk = dk + far_k[:, j * D:(j + 1) * D]
                    dv = dv + far_v[:, j * D:(j + 1) * D]
                dk_ref[rows, own] = dk
                dv_ref[rows, own] = dv
                if c > 0:
                    states[j] = states[j] + nn(qt_ref[own, rows], mg)


def finish_kernel(per, halves, me_ref, k_ref, v_ref, e0, e1, e2, e3, dk0, dk1, dv0, dv1, dk_hbm, dv_hbm, dk, dv, sems):
    tokens = k_ref.shape[0]
    me = me_ref[0] & (GROUP - 1)
    wide = per * D
    copies = []
    for s, e_ref in enumerate((e0, e1, e2, e3)):
        cols = slot_cols(me, s, wide)
        own = pl.ds((s % halves) * wide, wide)
        suffix = diagonal([e.astype(BF16) for e in heads_of(e_ref, per)])
        for c in range(tokens // ROWS):
            rows = pl.ds(c * ROWS, ROWS)
            dk[rows, cols] = ((dk0, dk1)[s // halves][rows, own] + nt(v_ref[rows, cols], suffix)).astype(BF16)
            dv[rows, cols] = ((dv0, dv1)[s // halves][rows, own] + nn(k_ref[rows, cols], suffix)).astype(BF16)
        for n, (src, dst) in enumerate(((dk, dk_hbm), (dv, dv_hbm))):
            copies.append(pltpu.make_async_copy(src.at[:, cols], dst.at[:, cols], sems.at[2 * s + n]))
            copies[-1].start()
    for copy in copies:
        copy.wait()


def swap(x, axis, n, mask):
    return lax.ppermute(x, axis, [(i, i ^ mask) for i in range(n)])


def total_kernel(*refs):
    *in_refs, out_ref = refs
    out_ref[...] = functools.reduce(lambda x, y: x + y, [r[...] for r in in_refs])


def before(a, b, ahead):
    return (a < b) if ahead else (a > b)


def masked(flag, x):
    return jnp.where(flag, x, 0.0)


def sums_kernel(ahead, steps, me_ref, *refs):
    me = me_ref[0]
    low = me & (GROUP - 1)
    got, others, outs = refs[:GROUP], refs[GROUP:GROUP + len(steps)], refs[GROUP + len(steps):]
    for j in range(outs[0].shape[0] // D):
        rows = pl.ds(j * D, D)
        carry = jnp.zeros((D, D), F32)
        for step, other in zip(steps, others):
            carry = carry + masked(before(me ^ step, me, ahead), other[rows, :])
        parts = [r[rows, :] for r in got]
        for s in range(GROUP):
            outs[s][rows, :] = carry + sum(
                masked(before(low ^ t, low ^ s, ahead), parts[t]) for t in range(GROUP) if t != s)


def scan_states(slots, me, n, ahead):
    got = [slots[0]] + [swap(slots[s], "ctx", n, s) for s in range(1, GROUP)]
    like = jax.ShapeDtypeStruct(slots[0].shape, F32)
    steps, others = [], []
    step = GROUP
    while step < n:
        (total,) = call(total_kernel, [like], got if step == GROUP else [total, others[-1]], 0)
        others.append(swap(total, "ctx", n, step))
        steps.append(step)
        step *= 2
    sums = call(
        functools.partial(sums_kernel, ahead, tuple(steps)), [like] * GROUP,
        [me, *got, *others], 0)
    return [sums[0]] + [swap(sums[s], "ctx", n, s) for s in range(1, GROUP)]


def shards(n, m, q, k, v, norm_gain, dy):
    return program(n, m, q, k, v, norm_gain, dy)


def program(n, m, q, k, v, norm_gain, dy):
    tokens, width = q.shape
    heads = width // D
    per = heads // GROUP
    halves = GROUP // 2
    half = width // 2
    full_width = HEADS * D
    me = lax.axis_index("ctx").astype(jnp.int32).reshape(1)
    gain = norm_gain.reshape(1, width)

    def shape(dtype, *dims):
        return jax.ShapeDtypeStruct(dims, dtype)

    state = shape(F32, per * D, D)
    wide = shape(F32, tokens, width)
    narrow = shape(BF16, tokens, width)
    unit = 2 * tokens * D * D
    part = functools.partial
    pairs = ((0, 1), (2, 3))

    q, k, v, dy = [pltpu.with_memory_space_constraint(x, pltpu.HBM) for x in (q, k, v, dy)]
    k, v, s1, s2, s3 = call(
        part(state_kernel, per), [narrow, narrow, state, state, state], [me, k, v],
        unit * heads, in_spaces=[SMEM, HBM, HBM], scratch=[pltpu.SemaphoreType.DMA((8,))])
    s0, q, dy = call(
        part(own_kernel, per), [state, narrow, narrow], [me, k, v, q, dy],
        unit * per, in_spaces=[SMEM, VMEM, VMEM, HBM, HBM], scratch=[pltpu.SemaphoreType.DMA((2,))])
    kept = [
        shape(F32, tokens, half), shape(BF16, half, tokens),
        shape(BF16, heads // 2, tokens, CHUNK), shape(F32, heads // 2, tokens // CHUNK * D, D)]
    fronts = [
        call(part(intra_kernel, pairs[i], per), kept, [me, q, k, v], 4 * unit * heads)
        for i in range(2)]
    intra, qt, pt, st = zip(*fronts)
    pre = scan_states([s0, s1, s2, s3], me, n, True)

    acc = pltpu.VMEM((tokens, D), F32)
    mixed, red = call(
        part(mix_kernel, per, halves), [wide, shape(F32, 2, tokens)],
        [me, q, dy, gain, *pre, *intra], unit * heads, scratch=(acc, acc))
    mask = 1
    while mask < m:
        red = red + swap(red, "fsdp", m, mask)
        mask *= 2

    mg, g0, g1, g2, g3 = call(
        part(grad_kernel, per, halves, full_width), [narrow] + [state] * 4,
        [me, *qt, mixed, dy, gain, red], unit * heads)
    whole = pltpu.VMEM((tokens, width), BF16)
    att, dq = call(
        part(query_kernel, per, halves, full_width), [narrow, narrow],
        [me, k, v, mg, mixed, gain, red, *pre, *st], 6 * unit * heads,
        out_spaces=[HBM, HBM], scratch=[whole, whole, pltpu.SemaphoreType.DMA((GROUP + 1,))], vmem=6)
    backs = [
        call(part(keyvalue_kernel, pairs[i], per), [shape(F32, tokens, half)] * 2,
             [me, q, k, v, mg, qt[i], pt[i]], 4 * unit * heads)
        for i in range(2)]
    dki, dvi = zip(*backs)
    suf = scan_states([g0, g1, g2, g3], me, n, False)
    dk, dv = call(
        part(finish_kernel, per, halves), [narrow, narrow],
        [me, k, v, *suf, *dki, *dvi], 2 * unit * heads,
        out_spaces=[HBM, HBM], scratch=[whole, whole, pltpu.SemaphoreType.DMA((2 * GROUP,))], vmem=6)
    return att, dq, dk, dv


def solution(mesh):
    in_specs = (P("ctx", "fsdp"), P("ctx", "fsdp"), P("ctx", "fsdp"), P("fsdp"), P("ctx", "fsdp"))
    out_specs = (P("ctx", "fsdp"),) * 4
    body = functools.partial(shards, mesh.shape["ctx"], mesh.shape["fsdp"])
    return jax.shard_map(body, mesh=mesh, in_specs=in_specs, out_specs=out_specs, check_vma=False)
```

time: 237 us -> 76.2 us (0.32)
  matrix products: 80.1 us -> 0 us
  waiting for transfers between devices: 88.7 us -> 17.4 us
  Pallas kernels: 0 us -> 35.4 us
  local copies, waits for them, and re-layouts: 33.1 us -> 0.01 us
  starting transfers between devices: 0.08 us -> 22.2 us
  other arithmetic: 14.3 us -> 0.01 us
  between operations: 14.2 us -> 0.97 us
  blocking collectives: 5.95 us -> 0 us
    all_gather x2 -> x0, waiting for transfers between devices: 88.7 us -> none  [the longest x1 53.7 us: earlier_states(): piece = lax.all_gather(local[None], 'ctx', axis=0, tiled=True)]
    dot_general x12 -> x0, matrix products: 80.1 us -> none  [the longest x1 11.4 us: shards(): jnp.einsum('hts,she->the', probs, values_here, preferred_element_type=f32)]
    pallas_call x0 -> x14, Pallas kernels: none -> 35.4 us  [call(): pl.pallas_call(kernel, out_shape=outs, in_specs=[pl.BlockSpec(memory_spac...]
    ppermute x0 -> x16, starting transfers between devices: none -> 22.2 us  [swap(): return lax.ppermute(x, axis, [(i, i ^ mask) for i in range(n)])]
    unnamed x22 -> x2, local copies, waits for them, and re-layouts: 17.6 us -> 0.01 us
    ppermute x0 -> x16, waiting for transfers between devices: none -> 17.4 us  [swap(): return lax.ppermute(x, axis, [(i, i ^ mask) for i in range(n)])]
    reshape x3 -> x1, local copies, waits for them, and re-layouts: 13.4 us -> 0.01 us  [program(): gain = norm_gain.reshape(1, width)]
    reduce_sum x3 -> x0, other arithmetic: 9.18 us -> none  [the longest x1 3.48 us: shards(): cross = lax.psum(jnp.sum(weighted * mixed, 1), 'fsdp')]
  transfers between devices with their start and end apart: 2 -> 16, of which waited for: 2 -> 8; matrix products, arithmetic and copies ran while one was open for 25% -> 0% of each run, Pallas kernels for 0% -> 33%
where the time goes in v2:
time: 76.2 us; the launch traced here: 76 us
  Pallas kernels  35.4 us (46%)
  starting transfers between devices  22.2 us (29%)
  waiting for transfers between devices  17.4 us (23%)
  between operations  0.97 us (1%)
    pallas_call x14, Pallas kernels, call(): pl.pallas_call(kernel, out_shape=outs, in_specs=[pl.BlockSpec(memory_spac...  35.4 us
    ppermute x16, starting transfers between devices, swap(): return lax.ppermute(x, axis, [(i, i ^ mask) for i in range(n)])  22.2 us
    ppermute x16, waiting for transfers between devices, swap(): return lax.ppermute(x, axis, [(i, i ^ mask) for i in range(n)])  17.4 us
  transfers between devices with their start and end apart: 16, of which 8 were waited for; matrix products, arithmetic and copies ran while one was open for 0% of the time, Pallas kernels for 33%

profile of v2, /device:TPU:0, one launch (start us, length us, event | category | flops | bytes accessed | tf_op | source)
XLA Modules:
  0.0 76.0 jit_solution(11605692272999193280)
XLA Ops:
  0.6 2.6 %shard_map.84 = (bf16[1024,1024]{1,0:T(8,128)(2,1)S(1)}, bf16[1024,1024]{1,0:T(8,128)(2,1)S(1)}, f32[256,128]{1,0:T(8,128)S(1)}, f32[256,128]{1,0:T(8,128)S(1)}, f32[256,128]{1,0:T(8,128)S(1)}) custom-call(s32[1]{0:T(128)} %bitcast.me_ref, bf16[1024,1024]{1,0:T(8,128)(2,1)} %k_hbm.1, bf16[1024,1024]{1,0:T(8,128)(2,1)} %v_hbm.1), custom_call_target="tpu_custom_call" | custom-call | flops 268435456 | bytes 4194308 | tf_op jit(solution)/shard_map/pallas_call | solution.py:61
  3.2 3.1 %collective-permute-start = (f32[256,128]{1,0:T(8,128)S(1)}, f32[256,128]{1,0:T(8,128)S(1)}, u32[]{:S(2)}, u32[]{:S(2)}) collective-permute-start(f32[256,128]{1,0:T(8,128)S(1)} %get-tuple-element.50), channel_id=1, source_target_pairs={{0,4},{4,0},{8,12},{12,8},{16,20},{20,16},{24,28},{28,24},{1,5},{5... | collective-permute-start | bytes 393224 | tf_op jit(solution)/shard_map/ppermute | solution.py:283
  6.3 1.6 %collective-permute-start.1 = (f32[256,128]{1,0:T(8,128)S(1)}, f32[256,128]{1,0:T(8,128)S(1)}, u32[]{:S(2)}, u32[]{:S(2)}) collective-permute-start(f32[256,128]{1,0:T(8,128)S(1)} %get-tuple-element.51), channel_id=1, source_target_pairs={{0,8},{4,12},{8,0},{12,4},{16,24},{20,28},{24,16},{28,20},{1,9},{5... | collective-permute-start | bytes 393224 | tf_op jit(solution)/shard_map/ppermute | solution.py:283
  7.9 0.0 collective-permute-start.2
  7.9 2.2 %shard_map.85 = (f32[256,128]{1,0:T(8,128)S(1)}, bf16[1024,1024]{1,0:T(8,128)(2,1)S(1)}, bf16[1024,1024]{1,0:T(8,128)(2,1)S(1)}) custom-call(s32[1]{0:T(128)} %bitcast.me_ref, bf16[1024,1024]{1,0:T(8,128)(2,1)S(1)} %get-tuple-element.43.k_ref, bf16[1024,1024]{1,0:T(8,128)(2,1)S(1)} %get-tuple-element.44.v_ref, bf16[1024,1024]{1,0:T(8,128)(2,1)} %q_hbm.1, ...), custom_call_target="tpu_custom_call" | custom-call | flops 67108864 | bytes 8388612 | tf_op jit(solution)/shard_map/pallas_call | solution.py:61
  10.1 0.0 collective-permute-done.refs_1_
  10.1 2.5 %collective-permute-done.1.refs_2_ = f32[256,128]{1,0:T(8,128)S(1)} collective-permute-done((f32[256,128]{1,0:T(8,128)S(1)}, f32[256,128]{1,0:T(8,128)S(1)}, u32[]{:S(2)}, u32[]{:S(2)}) %collective-permute-start.1) | collective-permute-done | bytes 131104 | tf_op jit(solution)/shard_map/ppermute | solution.py:283
  12.7 1.2 %collective-permute-done.2.refs_3_ = f32[256,128]{1,0:T(8,128)S(1)} collective-permute-done((f32[256,128]{1,0:T(8,128)S(1)}, f32[256,128]{1,0:T(8,128)S(1)}, u32[]{:S(2)}, u32[]{:S(2)}) %collective-permute-start.2) | collective-permute-done | bytes 131104 | tf_op jit(solution)/shard_map/ppermute | solution.py:283
  13.9 2.8 %collective-permute-start.3 = (f32[256,128]{1,0:T(8,128)S(1)}, f32[256,128]{1,0:T(8,128)S(1)}, u32[]{:S(2)}, u32[]{:S(2)}) collective-permute-start(f32[256,128]{1,0:T(8,128)S(1)} %shard_map.88), channel_id=1, source_target_pairs={{0,16},{4,20},{8,24},{12,28},{16,0},{20,4},{24,8},{28,12},{1,17},{... | collective-permute-start | bytes 393224 | tf_op jit(solution)/shard_map/ppermute | solution.py:283
  16.7 5.5 %collective-permute-done.3.refs_4_ = f32[256,128]{1,0:T(8,128)S(1)} collective-permute-done((f32[256,128]{1,0:T(8,128)S(1)}, f32[256,128]{1,0:T(8,128)S(1)}, u32[]{:S(2)}, u32[]{:S(2)}) %collective-permute-start.3) | collective-permute-done | bytes 131104 | tf_op jit(solution)/shard_map/ppermute | solution.py:283
  22.2 0.1 shard_map.89
  22.3 1.0 %collective-permute-start.4 = (f32[256,128]{1,0:T(8,128)S(1)}, f32[256,128]{1,0:T(8,128)S(1)}, u32[]{:S(2)}, u32[]{:S(2)}) collective-permute-start(f32[256,128]{1,0:T(8,128)S(1)} %get-tuple-element.54), channel_id=1, source_target_pairs={{0,4},{4,0},{8,12},{12,8},{16,20},{20,16},{24,28},{28,24},{1,5},{5... | collective-permute-start | bytes 393224 | tf_op jit(solution)/shard_map/ppermute | solution.py:283
  23.3 0.7 collective-permute-start.5
  24.0 1.8 %collective-permute-start.6 = (f32[256,128]{1,0:T(8,128)S(1)}, f32[256,128]{1,0:T(8,128)S(1)}, u32[]{:S(2)}, u32[]{:S(2)}) collective-permute-start(f32[256,128]{1,0:T(8,128)S(1)} %get-tuple-element.56), channel_id=1, source_target_pairs={{0,12},{4,8},{8,4},{12,0},{16,28},{20,24},{24,20},{28,16},{1,13},{... | collective-permute-start | bytes 393224 | tf_op jit(solution)/shard_map/ppermute | solution.py:283
  25.8 0.0 copy-start
  25.8 3.9 %shard_map.87 = (f32[1024,512]{1,0:T(8,128)S(1)}, bf16[512,1024]{1,0:T(8,128)(2,1)S(1)}, bf16[4,1024,256]{2,1,0:T(8,128)(2,1)S(1)}, f32[4,512,128]{2,1,0:T(8,128)S(1)}) custom-call(s32[1]{0:T(128)} %bitcast.me_ref, bf16[1024,1024]{1,0:T(8,128)(2,1)S(1)} %get-tuple-element.45.q_ref, bf16[1024,1024]{1,0:T(8,128)(2,1)S(1)} %get-tuple-element.43.k_ref, ...), custom_call_target="tpu_custom_call" | custom-call | flops 1073741824 | bytes 6291460 | tf_op jit(solution)/shard_map/pallas_call | solution.py:61
  29.8 0.0 copy-done
  29.8 4.0 %shard_map.86 = (f32[1024,512]{1,0:T(8,128)S(1)}, bf16[512,1024]{1,0:T(8,128)(2,1)S(1)}, bf16[4,1024,256]{2,1,0:T(8,128)(2,1)S(1)}, f32[4,512,128]{2,1,0:T(8,128)S(1)}) custom-call(s32[1]{0:T(128)} %bitcast.me_ref, bf16[1024,1024]{1,0:T(8,128)(2,1)S(1)} %get-tuple-element.45.q_ref, bf16[1024,1024]{1,0:T(8,128)(2,1)S(1)} %get-tuple-element.43.k_ref, ...), custom_call_target="tpu_custom_call" | custom-call | flops 1073741824 | bytes 6291460 | tf_op jit(solution)/shard_map/pallas_call | solution.py:61
  33.8 0.0 collective-permute-done.4.e1
  33.8 0.0 collective-permute-done.5.e2
  33.8 0.0 collective-permute-done.6.e3
  33.8 2.3 %shard_map.90 = (f32[1024,1024]{1,0:T(8,128)S(1)}, f32[2,1024]{1,0:T(2,128)S(1)}) custom-call(s32[1]{0:T(128)} %bitcast.me_ref, bf16[1024,1024]{1,0:T(8,128)(2,1)S(1)} %get-tuple-element.45.q_ref, bf16[1024,1024]{1,0:T(8,128)(2,1)S(1)} %get-tuple-element.48.dy_ref, bf16[1,1024]{1,0:T(2,128)(2,1)S(1)} %reshape.15.gain_ref, ...), custom_call_target="tpu_custom_call" | custom-call | flops 268435456 | bytes 8914948 | tf_op jit(solution)/shard_map/pallas_call | solution.py:61
  36.1 0.0 collective-permute-start.7
  36.1 1.2 %collective-permute-done.7 = f32[2,1024]{1,0:T(2,128)S(1)} collective-permute-done((f32[2,1024]{1,0:T(2,128)S(1)}, f32[2,1024]{1,0:T(2,128)S(1)}, u32[]{:S(2)}, u32[]{:S(2)}) %collective-permute-start.7) | collective-permute-done | bytes 8224 | tf_op jit(solution)/shard_map/ppermute | solution.py:283
  37.3 1.5 %collective-permute-start.8 = (f32[2,1024]{1,0:T(2,128)S(1)}, f32[2,1024]{1,0:T(2,128)S(1)}, u32[]{:S(2)}, u32[]{:S(2)}) collective-permute-start(f32[2,1024]{1,0:T(2,128)S(1)} %add.6), channel_id=1, source_target_pairs={{0,2},{1,3},{2,0},{3,1},{4,6},{5,7},{6,4},{7,5},{8,10},{9,11},{10,... | collective-permute-start | bytes 24584 | tf_op jit(solution)/shard_map/ppermute | solution.py:283
  38.9 2.1 %collective-permute-done.8 = f32[2,1024]{1,0:T(2,128)S(1)} collective-permute-done((f32[2,1024]{1,0:T(2,128)S(1)}, f32[2,1024]{1,0:T(2,128)S(1)}, u32[]{:S(2)}, u32[]{:S(2)}) %collective-permute-start.8) | collective-permute-done | bytes 8224 | tf_op jit(solution)/shard_map/ppermute | solution.py:283
  41.0 2.1 %shard_map.91 = (bf16[1024,1024]{1,0:T(8,128)(2,1)S(1)}, f32[256,128]{1,0:T(8,128)S(1)}, f32[256,128]{1,0:T(8,128)S(1)}, f32[256,128]{1,0:T(8,128)S(1)}, f32[256,128]{1,0:T(8,128)S(1)}) custom-call(s32[1]{0:T(128)} %bitcast.me_ref, bf16[512,1024]{1,0:T(8,128)(2,1)S(1)} %get-tuple-element.46.qt0.qt_ref, bf16[512,1024]{1,0:T(8,128)(2,1)S(1)} %get-tuple-element.47.qt1.qt_ref, ...), custom_call_target="tpu_custom_call" | custom-call | flops 268435456 | bytes 8398852 | tf_op jit(solution)/shard_map/pallas_call | solution.py:61
  43.0 1.1 %collective-permute-start.9 = (f32[256,128]{1,0:T(8,128)S(1)}, f32[256,128]{1,0:T(8,128)S(1)}, u32[]{:S(2)}, u32[]{:S(2)}) collective-permute-start(f32[256,128]{1,0:T(8,128)S(1)} %get-tuple-element.67), channel_id=1, source_target_pairs={{0,4},{4,0},{8,12},{12,8},{16,20},{20,16},{24,28},{28,24},{1,5},{5... | collective-permute-start | bytes 393224 | tf_op jit(solution)/shard_map/ppermute | solution.py:283
  44.1 0.6 collective-permute-start.10
  44.7 1.9 %collective-permute-start.11 = (f32[256,128]{1,0:T(8,128)S(1)}, f32[256,128]{1,0:T(8,128)S(1)}, u32[]{:S(2)}, u32[]{:S(2)}) collective-permute-start(f32[256,128]{1,0:T(8,128)S(1)} %get-tuple-element.69), channel_id=1, source_target_pairs={{0,12},{4,8},{8,4},{12,0},{16,28},{20,24},{24,20},{28,16},{1,13},{... | collective-permute-start | bytes 393224 | tf_op jit(solution)/shard_map/ppermute | solution.py:283
  46.6 2.9 %collective-permute-done.9.refs_1_ = f32[256,128]{1,0:T(8,128)S(1)} collective-permute-done((f32[256,128]{1,0:T(8,128)S(1)}, f32[256,128]{1,0:T(8,128)S(1)}, u32[]{:S(2)}, u32[]{:S(2)}) %collective-permute-start.9) | collective-permute-done | bytes 131104 | tf_op jit(solution)/shard_map/ppermute | solution.py:283
  49.5 0.2 collective-permute-done.10.refs_2_
  49.6 1.9 %collective-permute-done.11.refs_3_ = f32[256,128]{1,0:T(8,128)S(1)} collective-permute-done((f32[256,128]{1,0:T(8,128)S(1)}, f32[256,128]{1,0:T(8,128)S(1)}, u32[]{:S(2)}, u32[]{:S(2)}) %collective-permute-start.11) | collective-permute-done | bytes 131104 | tf_op jit(solution)/shard_map/ppermute | solution.py:283
  51.5 2.5 %collective-permute-start.12 = (f32[256,128]{1,0:T(8,128)S(1)}, f32[256,128]{1,0:T(8,128)S(1)}, u32[]{:S(2)}, u32[]{:S(2)}) collective-permute-start(f32[256,128]{1,0:T(8,128)S(1)} %shard_map.93), channel_id=1, source_target_pairs={{0,16},{4,20},{8,24},{12,28},{16,0},{20,4},{24,8},{28,12},{1,17},{... | collective-permute-start | bytes 393224 | tf_op jit(solution)/shard_map/ppermute | solution.py:283
  54.1 4.6 %shard_map.96 = (f32[1024,512]{1,0:T(8,128)S(1)}, f32[1024,512]{1,0:T(8,128)S(1)}) custom-call(s32[1]{0:T(128)} %bitcast.me_ref, bf16[1024,1024]{1,0:T(8,128)(2,1)S(1)} %get-tuple-element.45.q_ref, bf16[1024,1024]{1,0:T(8,128)(2,1)S(1)} %get-tuple-element.43.k_ref, bf16[1024,1024]{1,0:T(8,128)(2,1)S(1)} %get-tuple-element.44.v_ref, ...), custom_call_target="tpu_custom_call" | custom-call | flops 1073741824 | bytes 11534340 | tf_op jit(solution)/shard_map/pallas_call | solution.py:61
  58.7 4.6 %shard_map.95 = (f32[1024,512]{1,0:T(8,128)S(1)}, f32[1024,512]{1,0:T(8,128)S(1)}) custom-call(s32[1]{0:T(128)} %bitcast.me_ref, bf16[1024,1024]{1,0:T(8,128)(2,1)S(1)} %get-tuple-element.45.q_ref, bf16[1024,1024]{1,0:T(8,128)(2,1)S(1)} %get-tuple-element.43.k_ref, bf16[1024,1024]{1,0:T(8,128)(2,1)S(1)} %get-tuple-element.44.v_ref, ...), custom_call_target="tpu_custom_call" | custom-call | flops 1073741824 | bytes 11534340 | tf_op jit(solution)/shard_map/pallas_call | solution.py:61
  63.4 0.0 collective-permute-done.12.refs_4_
  63.4 0.1 shard_map.94
  63.5 0.9 %collective-permute-start.13 = (f32[256,128]{1,0:T(8,128)S(1)}, f32[256,128]{1,0:T(8,128)S(1)}, u32[]{:S(2)}, u32[]{:S(2)}) collective-permute-start(f32[256,128]{1,0:T(8,128)S(1)} %get-tuple-element.71), channel_id=1, source_target_pairs={{0,4},{4,0},{8,12},{12,8},{16,20},{20,16},{24,28},{28,24},{1,5},{5... | collective-permute-start | bytes 393224 | tf_op jit(solution)/shard_map/ppermute | solution.py:283
  64.4 1.7 %collective-permute-start.14 = (f32[256,128]{1,0:T(8,128)S(1)}, f32[256,128]{1,0:T(8,128)S(1)}, u32[]{:S(2)}, u32[]{:S(2)}) collective-permute-start(f32[256,128]{1,0:T(8,128)S(1)} %get-tuple-element.72), channel_id=1, source_target_pairs={{0,8},{4,12},{8,0},{12,4},{16,24},{20,28},{24,16},{28,20},{1,9},{5... | collective-permute-start | bytes 393224 | tf_op jit(solution)/shard_map/ppermute | solution.py:283
  66.1 1.0 %collective-permute-start.15 = (f32[256,128]{1,0:T(8,128)S(1)}, f32[256,128]{1,0:T(8,128)S(1)}, u32[]{:S(2)}, u32[]{:S(2)}) collective-permute-start(f32[256,128]{1,0:T(8,128)S(1)} %get-tuple-element.73), channel_id=1, source_target_pairs={{0,12},{4,8},{8,4},{12,0},{16,28},{20,24},{24,20},{28,16},{1,13},{... | collective-permute-start | bytes 393224 | tf_op jit(solution)/shard_map/ppermute | solution.py:283
  67.1 5.8 %shard_map.92 = (bf16[1024,1024]{1,0:T(8,128)(2,1)}, bf16[1024,1024]{1,0:T(8,128)(2,1)}) custom-call(s32[1]{0:T(128)} %bitcast.me_ref, bf16[1024,1024]{1,0:T(8,128)(2,1)S(1)} %get-tuple-element.43.k_ref, bf16[1024,1024]{1,0:T(8,128)(2,1)S(1)} %get-tuple-element.44.v_ref, bf16[1024,1024]{1,0:T(8,128)(2,1)S(1)} %get-tuple-element.61.mg_ref, ...), custom_call_target="tpu_custom_call" | custom-call | flops 1610612736 | bytes 13117444 | tf_op jit(solution)/shard_map/pallas_call | solution.py:61
  72.8 0.0 collective-permute-done.13.e1
  72.8 0.0 collective-permute-done.14.e2
  72.8 0.0 collective-permute-done.15.e3
  72.8 3.0 %shard_map.97 = (bf16[1024,1024]{1,0:T(8,128)(2,1)}, bf16[1024,1024]{1,0:T(8,128)(2,1)}) custom-call(s32[1]{0:T(128)} %bitcast.me_ref, bf16[1024,1024]{1,0:T(8,128)(2,1)S(1)} %get-tuple-element.43.k_ref, bf16[1024,1024]{1,0:T(8,128)(2,1)S(1)} %get-tuple-element.44.v_ref, f32[256,128]{1,0:T(8,128)S(1)} %get-tuple-element.70.e0, ...), custom_call_target="tpu_custom_call" | custom-call | flops 536870912 | bytes 13107204 | tf_op jit(solution)/shard_map/pallas_call | solution.py:61
  (5 shorter events, 0.1 us)
Async XLA Ops:
  3.2 6.9 %collective-permute-start = (f32[256,128]{1,0:T(8,128)S(1)}, f32[256,128]{1,0:T(8,128)S(1)}, u32[]{:S(2)}, u32[]{:S(2)}) collective-permute-start(f32[256,128]{1,0:T(8,128)S(1)} %get-tuple-element.50), channel_id=1, source_target_pairs={{0,4},{4,0},{8,12},{12,8},{16,20},{20,16},{24,28},{28,24},{1,5},{5... | collective-permute-start | bytes 393224 | tf_op jit(solution)/shard_map/ppermute | solution.py:283
  6.3 6.4 %collective-permute-start.1 = (f32[256,128]{1,0:T(8,128)S(1)}, f32[256,128]{1,0:T(8,128)S(1)}, u32[]{:S(2)}, u32[]{:S(2)}) collective-permute-start(f32[256,128]{1,0:T(8,128)S(1)} %get-tuple-element.51), channel_id=1, source_target_pairs={{0,8},{4,12},{8,0},{12,4},{16,24},{20,28},{24,16},{28,20},{1,9},{5... | collective-permute-start | bytes 393224 | tf_op jit(solution)/shard_map/ppermute | solution.py:283
  7.9 6.0 %collective-permute-start.2 = (f32[256,128]{1,0:T(8,128)S(1)}, f32[256,128]{1,0:T(8,128)S(1)}, u32[]{:S(2)}, u32[]{:S(2)}) collective-permute-start(f32[256,128]{1,0:T(8,128)S(1)} %get-tuple-element.52), channel_id=1, source_target_pairs={{0,12},{4,8},{8,4},{12,0},{16,28},{20,24},{24,20},{28,16},{1,13},{... | collective-permute-start | bytes 393224 | tf_op jit(solution)/shard_map/ppermute | solution.py:283
  13.9 8.3 %collective-permute-start.3 = (f32[256,128]{1,0:T(8,128)S(1)}, f32[256,128]{1,0:T(8,128)S(1)}, u32[]{:S(2)}, u32[]{:S(2)}) collective-permute-start(f32[256,128]{1,0:T(8,128)S(1)} %shard_map.88), channel_id=1, source_target_pairs={{0,16},{4,20},{8,24},{12,28},{16,0},{20,4},{24,8},{28,12},{1,17},{... | collective-permute-start | bytes 393224 | tf_op jit(solution)/shard_map/ppermute | solution.py:283
  22.3 11.5 %collective-permute-start.4 = (f32[256,128]{1,0:T(8,128)S(1)}, f32[256,128]{1,0:T(8,128)S(1)}, u32[]{:S(2)}, u32[]{:S(2)}) collective-permute-start(f32[256,128]{1,0:T(8,128)S(1)} %get-tuple-element.54), channel_id=1, source_target_pairs={{0,4},{4,0},{8,12},{12,8},{16,20},{20,16},{24,28},{28,24},{1,5},{5... | collective-permute-start | bytes 393224 | tf_op jit(solution)/shard_map/ppermute | solution.py:283
  23.3 10.4 %collective-permute-start.5 = (f32[256,128]{1,0:T(8,128)S(1)}, f32[256,128]{1,0:T(8,128)S(1)}, u32[]{:S(2)}, u32[]{:S(2)}) collective-permute-start(f32[256,128]{1,0:T(8,128)S(1)} %get-tuple-element.55), channel_id=1, source_target_pairs={{0,8},{4,12},{8,0},{12,4},{16,24},{20,28},{24,16},{28,20},{1,9},{5... | collective-permute-start | bytes 393224 | tf_op jit(solution)/shard_map/ppermute | solution.py:283
  24.0 9.8 %collective-permute-start.6 = (f32[256,128]{1,0:T(8,128)S(1)}, f32[256,128]{1,0:T(8,128)S(1)}, u32[]{:S(2)}, u32[]{:S(2)}) collective-permute-start(f32[256,128]{1,0:T(8,128)S(1)} %get-tuple-element.56), channel_id=1, source_target_pairs={{0,12},{4,8},{8,4},{12,0},{16,28},{20,24},{24,20},{28,16},{1,13},{... | collective-permute-start | bytes 393224 | tf_op jit(solution)/shard_map/ppermute | solution.py:283
  25.8 3.9 %copy-start = (bf16[1024]{0:T(1024)(128)(2,1)S(1)}, bf16[1024]{0:T(1024)(128)(2,1)}, u32[]{:S(2)}) copy-start(bf16[1024]{0:T(1024)(128)(2,1)} %param.8) | copy-start | bytes 6148
  36.1 1.2 %collective-permute-start.7 = (f32[2,1024]{1,0:T(2,128)S(1)}, f32[2,1024]{1,0:T(2,128)S(1)}, u32[]{:S(2)}, u32[]{:S(2)}) collective-permute-start(f32[2,1024]{1,0:T(2,128)S(1)} %get-tuple-element.60), channel_id=1, source_target_pairs={{0,1},{1,0},{2,3},{3,2},{4,5},{5,4},{6,7},{7,6},{8,9},{9,8},{10,11... | collective-permute-start | bytes 24584 | tf_op jit(solution)/shard_map/ppermute | solution.py:283
  37.3 3.7 %collective-permute-start.8 = (f32[2,1024]{1,0:T(2,128)S(1)}, f32[2,1024]{1,0:T(2,128)S(1)}, u32[]{:S(2)}, u32[]{:S(2)}) collective-permute-start(f32[2,1024]{1,0:T(2,128)S(1)} %add.6), channel_id=1, source_target_pairs={{0,2},{1,3},{2,0},{3,1},{4,6},{5,7},{6,4},{7,5},{8,10},{9,11},{10,... | collective-permute-start | bytes 24584 | tf_op jit(solution)/shard_map/ppermute | solution.py:283
  43.0 6.4 %collective-permute-start.9 = (f32[256,128]{1,0:T(8,128)S(1)}, f32[256,128]{1,0:T(8,128)S(1)}, u32[]{:S(2)}, u32[]{:S(2)}) collective-permute-start(f32[256,128]{1,0:T(8,128)S(1)} %get-tuple-element.67), channel_id=1, source_target_pairs={{0,4},{4,0},{8,12},{12,8},{16,20},{20,16},{24,28},{28,24},{1,5},{5... | collective-permute-start | bytes 393224 | tf_op jit(solution)/shard_map/ppermute | solution.py:283
  44.1 5.5 %collective-permute-start.10 = (f32[256,128]{1,0:T(8,128)S(1)}, f32[256,128]{1,0:T(8,128)S(1)}, u32[]{:S(2)}, u32[]{:S(2)}) collective-permute-start(f32[256,128]{1,0:T(8,128)S(1)} %get-tuple-element.68), channel_id=1, source_target_pairs={{0,8},{4,12},{8,0},{12,4},{16,24},{20,28},{24,16},{28,20},{1,9},{5... | collective-permute-start | bytes 393224 | tf_op jit(solution)/shard_map/ppermute | solution.py:283
  44.7 6.8 %collective-permute-start.11 = (f32[256,128]{1,0:T(8,128)S(1)}, f32[256,128]{1,0:T(8,128)S(1)}, u32[]{:S(2)}, u32[]{:S(2)}) collective-permute-start(f32[256,128]{1,0:T(8,128)S(1)} %get-tuple-element.69), channel_id=1, source_target_pairs={{0,12},{4,8},{8,4},{12,0},{16,28},{20,24},{24,20},{28,16},{1,13},{... | collective-permute-start | bytes 393224 | tf_op jit(solution)/shard_map/ppermute | solution.py:283
  51.5 11.8 %collective-permute-start.12 = (f32[256,128]{1,0:T(8,128)S(1)}, f32[256,128]{1,0:T(8,128)S(1)}, u32[]{:S(2)}, u32[]{:S(2)}) collective-permute-start(f32[256,128]{1,0:T(8,128)S(1)} %shard_map.93), channel_id=1, source_target_pairs={{0,16},{4,20},{8,24},{12,28},{16,0},{20,4},{24,8},{28,12},{1,17},{... | collective-permute-start | bytes 393224 | tf_op jit(solution)/shard_map/ppermute | solution.py:283
  63.5 9.3 %collective-permute-start.13 = (f32[256,128]{1,0:T(8,128)S(1)}, f32[256,128]{1,0:T(8,128)S(1)}, u32[]{:S(2)}, u32[]{:S(2)}) collective-permute-start(f32[256,128]{1,0:T(8,128)S(1)} %get-tuple-element.71), channel_id=1, source_target_pairs={{0,4},{4,0},{8,12},{12,8},{16,20},{20,16},{24,28},{28,24},{1,5},{5... | collective-permute-start | bytes 393224 | tf_op jit(solution)/shard_map/ppermute | solution.py:283
  64.4 8.4 %collective-permute-start.14 = (f32[256,128]{1,0:T(8,128)S(1)}, f32[256,128]{1,0:T(8,128)S(1)}, u32[]{:S(2)}, u32[]{:S(2)}) collective-permute-start(f32[256,128]{1,0:T(8,128)S(1)} %get-tuple-element.72), channel_id=1, source_target_pairs={{0,8},{4,12},{8,0},{12,4},{16,24},{20,28},{24,16},{28,20},{1,9},{5... | collective-permute-start | bytes 393224 | tf_op jit(solution)/shard_map/ppermute | solution.py:283
  66.1 6.7 %collective-permute-start.15 = (f32[256,128]{1,0:T(8,128)S(1)}, f32[256,128]{1,0:T(8,128)S(1)}, u32[]{:S(2)}, u32[]{:S(2)}) collective-permute-start(f32[256,128]{1,0:T(8,128)S(1)} %get-tuple-element.73), channel_id=1, source_target_pairs={{0,12},{4,8},{8,4},{12,0},{16,28},{20,24},{24,20},{28,16},{1,13},{... | collective-permute-start | bytes 393224 | tf_op jit(solution)/shard_map/ppermute | solution.py:283
